TPU v7x, 128 devices: a whole 4x4x4 slice. The times are simulated.
128 devices in a mesh: grp: 4 (over y), blk: 8 (over z, x_lo), ch: 4 (over x_hi, core).
Axes of the slice: x: 4 (x_hi: 2, x_lo: 2; x = x_hi * 2 + x_lo), y: 4, z: 4, core: 2. Of those that a mesh axis runs over, the one named last changes fastest.
Arguments:
- gate_in: bfloat16 [12288, 1024], P(('grp', 'blk'), 'ch'), parts along dimension 1, may hold values from -6 to 6
- value_in: bfloat16 [12288, 1024], P(('grp', 'blk'), 'ch'), parts along dimension 1, may hold values from -6 to 6
- gate_out: bfloat16 [12288, 1024], P(('grp', 'blk'), 'ch'), parts along dimension 1, may hold values from -6 to 6
- filter_taps: float32 [12288, 1024], P(('grp', 'blk'), 'ch'), parts along dimension 1, may hold values from -6 to 6
- skip_gain: float32 [1024], P('ch'), parts along dimension 0, may hold values from -4 to 4
- cotangent: bfloat16 [12288, 1024], P(('grp', 'blk'), 'ch'), parts along dimension 1, may hold values from -10 to 10
Outputs:
- grad_gate_in: bfloat16 [12288, 1024], P(('grp', 'blk'), 'ch'), parts along dimension 1
- grad_value_in: bfloat16 [12288, 1024], P(('grp', 'blk'), 'ch'), parts along dimension 1
- grad_gate_out: bfloat16 [12288, 1024], P(('grp', 'blk'), 'ch'), parts along dimension 1
- grad_filter: float32 [12288, 1024], P(('grp', 'blk'), 'ch'), parts along dimension 1
- grad_skip: float32 [1024], P('ch'), parts along dimension 0
There are 4 independent parts, one for each index of `ch`. A program takes and returns all parts, laid end to end along the dimension named above; each array names one. Nothing has to cross between parts.
All inputs are finite; a program needn't handle non-finite values.
Results may differ from a plain program's by a relative error of at most 0.001.
Values sent between devices are 32-bit elements; how exact they have to be, the bound alone decides.
No kernel may reach another device: no remote copies, remote signals or barrier semaphores. Data moves between devices by JAX's collectives and lax.ppermute only.
A program may use at most 128 MiB of HBM per device.

v0:
```python
import math

import jax
import jax.numpy as jnp
from jax import lax
from jax.sharding import PartitionSpec as P

SUB = 32


HIGHEST = lax.Precision.HIGHEST


def transform(real_part, imag_part, sequence_dimension, sign):
    length = real_part.shape[sequence_dimension]
    index = jnp.arange(length, dtype=jnp.int32)
    theta = 2.0 * math.pi / length * (index[:, None] * index[None, :] % length).astype(jnp.float32)
    cosine = jnp.cos(theta)
    sine = sign * jnp.sin(theta)
    letters = "abcdefg"[: real_part.ndim]
    form = (
        letters
        + ","
        + letters[sequence_dimension]
        + "z->"
        + letters[:sequence_dimension]
        + "z"
        + letters[sequence_dimension + 1 :]
    )

    def contract(values, table):
        return jnp.einsum(form, values, table, precision=HIGHEST)

    new_real = contract(real_part, cosine) + contract(imag_part, sine)
    new_imag = contract(imag_part, cosine) - contract(real_part, sine)
    return (new_real, new_imag)


def twist(real_part, imag_part, theta, sign):
    cosine = jnp.cos(theta)
    sine = sign * jnp.sin(theta)
    return (cosine * real_part + sine * imag_part, cosine * imag_part - sine * real_part)


def inner_angles(outer, length):
    first = jnp.arange(outer, dtype=jnp.int32)[:, None]
    second = jnp.arange(SUB, dtype=jnp.int32)[None, :]
    return 2.0 * math.pi / length * (first * second % length).astype(jnp.float32)


def local_forward(real_part, imag_part):
    shape = real_part.shape
    outer = shape[2] // SUB
    real_part = real_part.reshape(shape[0], shape[1], outer, SUB, shape[3])
    imag_part = imag_part.reshape(shape[0], shape[1], outer, SUB, shape[3])
    real_part, imag_part = transform(real_part, imag_part, 2, 1.0)
    theta = inner_angles(outer, shape[2])[:, :, None]
    real_part, imag_part = twist(real_part, imag_part, theta, 1.0)
    return transform(real_part, imag_part, 3, 1.0)


def local_inverse(real_part, imag_part):
    shape = real_part.shape
    real_part, imag_part = transform(real_part, imag_part, 3, -1.0)
    theta = inner_angles(shape[2], shape[2] * SUB)[:, :, None]
    real_part, imag_part = twist(real_part, imag_part, theta, -1.0)
    real_part, imag_part = transform(real_part, imag_part, 2, -1.0)
    full = (shape[0], shape[1], shape[2] * SUB, shape[4])
    return (real_part.reshape(full), imag_part.reshape(full))


def across_whole(stacked, sign):
    received = lax.all_to_all(stacked, ("grp", "blk"), split_axis=3, concat_axis=3, tiled=True)
    pieces = lax.axis_size(("grp", "blk"))
    shape = received.shape
    split = received.reshape(shape[0], shape[1], shape[2], pieces, shape[3] // pieces, shape[4])
    real_part, imag_part = transform(split[0], split[1], 2, sign)
    joined = jnp.stack([real_part, imag_part]).reshape(shape)
    return lax.all_to_all(joined, ("grp", "blk"), split_axis=3, concat_axis=3, tiled=True)


def body(gate_in, value_in, gate_out, filter_taps, skip_gain, cotangent):
    rows = gate_in.shape[0]
    first = gate_in.astype(jnp.float32)
    value = value_in.astype(jnp.float32)
    second = gate_out.astype(jnp.float32)
    grad = cotangent.astype(jnp.float32)
    mixed = first * value
    upstream = grad * second
    devices = lax.axis_size(("grp", "blk"))
    total = 2 * devices * rows
    block = lax.axis_index(("grp", "blk"))
    signals = jnp.stack([mixed, filter_taps, upstream])
    turn = math.pi / devices * block.astype(jnp.float32)
    real_part = jnp.stack([signals, signals * jnp.cos(turn)], axis=1)
    imag_part = jnp.stack([jnp.zeros_like(signals), -signals * jnp.sin(turn)], axis=1)
    stacked = jnp.stack([real_part, imag_part])
    stacked = across_whole(stacked, 1.0)
    spectral_rows = 2 * block + jnp.arange(2, dtype=jnp.int32)
    positions = jnp.arange(rows, dtype=jnp.int32)
    theta = (
        2.0
        * math.pi
        / total
        * (spectral_rows[:, None] * positions[None, :] % total).astype(jnp.float32)
    )
    theta = theta[None, :, :, None]
    real_part, imag_part = twist(stacked[0], stacked[1], theta, 1.0)
    real_part, imag_part = local_forward(real_part, imag_part)
    mixed_real, filter_real, up_real = (real_part[0], real_part[1], real_part[2])
    mixed_imag, filter_imag, up_imag = (imag_part[0], imag_part[1], imag_part[2])
    prod_real = jnp.stack(
        [
            filter_real * mixed_real - filter_imag * mixed_imag,
            filter_real * up_real + filter_imag * up_imag,
            mixed_real * up_real + mixed_imag * up_imag,
        ]
    )
    prod_imag = jnp.stack(
        [
            filter_real * mixed_imag + filter_imag * mixed_real,
            filter_real * up_imag - filter_imag * up_real,
            mixed_real * up_imag - mixed_imag * up_real,
        ]
    )
    real_part, imag_part = local_inverse(prod_real, prod_imag)
    real_part, imag_part = twist(real_part, imag_part, theta, -1.0)
    stacked = jnp.stack([real_part, imag_part])
    stacked = across_whole(stacked, -1.0)
    results = (
        stacked[0][:, 0] + jnp.cos(turn) * stacked[0][:, 1] - jnp.sin(turn) * stacked[1][:, 1]
    ) / total
    conv, back, lagged = (results[0], results[1], results[2])
    scale = 1.0 / math.sqrt(devices * rows)
    gain = skip_gain[None, :]
    grad_gate_out = (grad * (conv + gain * mixed)).astype(jnp.bfloat16)
    grad_mixed = back + gain * upstream
    grad_gate_in = (grad_mixed * value).astype(jnp.bfloat16)
    grad_value_in = (grad_mixed * first).astype(jnp.bfloat16)
    grad_filter = lagged * scale
    grad_skip = lax.psum(jnp.sum(upstream * mixed, axis=0), ("grp", "blk")) * scale
    return (grad_gate_in, grad_value_in, grad_gate_out, grad_filter, grad_skip)


def solution(mesh):
    placed = (
        P(("grp", "blk"), "ch"),
        P(("grp", "blk"), "ch"),
        P(("grp", "blk"), "ch"),
        P(("grp", "blk"), "ch"),
        P("ch"),
        P(("grp", "blk"), "ch"),
    )
    return jax.shard_map(
        body,
        mesh=mesh,
        in_specs=placed,
        out_specs=(
            P(("grp", "blk"), "ch"),
            P(("grp", "blk"), "ch"),
            P(("grp", "blk"), "ch"),
            P(("grp", "blk"), "ch"),
            P("ch"),
        ),
        check_vma=False,
    )
```

profile of v0, /device:TPU:0, one launch (start us, length us, event | category | flops | bytes accessed | tf_op | source)
XLA Modules:
  0.0 463.6 jit_solution(3017034531989703597)
XLA Ops:
  0.8 1.1 fusion.77
  1.9 1.1 fusion.79
  3.1 0.2 fusion.69
  3.3 0.5 maximum_bitcast_fusion
  3.8 0.6 pad_maximum_fusion
  4.3 3.6 copy.103
  8.0 66.6 %all_to_all.20 = f32[2,3,2,384,256]{4,2,1,0,3:T(2,128)S(1)} all-to-all(f32[2,3,2,384,256]{4,2,1,0,3:T(2,128)S(1)} %copy.103), channel_id=1, replica_groups=mesh['grp'=4,'blk'=8,'ch'=4] {'grp','blk'}, dimensions={3} | all-to-all | bytes 9437184 | tf_op jit(solution)/shard_map/all_to_all | solution.py:73
  74.6 1.6 fusion.296
  76.2 2.6 fusion.28
  78.8 2.6 fusion.26
  81.5 2.6 add_bitcast_fusion.4
  84.1 1.8 copy.108
  85.9 2.8 subtract_bitcast_fusion.4
  88.7 1.8 copy.111
  90.6 2.2 pad_maximum_fusion.1
  92.8 3.8 copy.112
  96.6 5.3 %all-to-all-start.1 = ((f32[2,3,2,384,256]{4,2,1,0,3:T(2,128)}), f32[2,3,2,384,256]{4,2,1,0,3:T(2,128)}, u32[]{:S(2)}, u32[]{:S(2)}) async-start(f32[2,3,2,384,256]{4,2,1,0,3:T(2,128)} %copy.112), calls=%async_computation.1 | async-start | bytes 9437184 | tf_op jit(solution)/shard_map/all_to_all | solution.py:79
  102.5 69.9 %all-to-all-done.1 = f32[2,3,2,384,256]{4,2,1,0,3:T(2,128)} async-done(((f32[2,3,2,384,256]{4,2,1,0,3:T(2,128)}), f32[2,3,2,384,256]{4,2,1,0,3:T(2,128)}, u32[]{:S(2)}, u32[]{:S(2)}) %all-to-all-start.1) | async-done | bytes 4718624 | tf_op jit(solution)/shard_map/all_to_all | solution.py:79
  172.4 4.0 fusion.295
  176.5 0.2 copy.156
  176.7 0.2 copy.157
  176.9 0.7 multiply_add_fusion.1
  177.6 4.0 fusion.10
  181.7 3.9 fusion.8
  185.6 4.2 fusion.34
  189.8 4.6 add_bitcast_fusion.1
  194.4 3.4 fusion.46
  197.8 3.6 fusion.44
  201.4 3.5 add_bitcast_fusion.3
  205.0 3.5 subtract_bitcast_fusion.3
  208.4 0.5 multiply_add_fusion.4
  208.9 0.6 multiply_subtract_fusion.4
  209.6 2.6 fusion.64
  212.2 2.2 fusion.65
  214.4 2.3 convolution_add_fusion
  216.7 2.8 fusion.16
  219.5 4.0 fusion.2
  223.6 4.2 fusion
  227.8 4.0 add_bitcast_fusion
  231.8 1.4 copy.126
  233.2 4.4 subtract_bitcast_fusion
  237.6 1.4 copy.129
  238.9 0.6 multiply_add_fusion
  239.5 0.3 pad_maximum_fusion.2
  239.8 3.6 copy.130
  243.5 58.6 %all_to_all.21 = f32[2,3,2,384,256]{4,2,1,0,3:T(2,128)S(1)} all-to-all(f32[2,3,2,384,256]{4,2,1,0,3:T(2,128)S(1)} %copy.130), channel_id=1, replica_groups=mesh['grp'=4,'blk'=8,'ch'=4] {'grp','blk'}, dimensions={3} | all-to-all | bytes 9437184 | tf_op jit(solution)/shard_map/all_to_all | solution.py:73
  302.1 1.6 fusion.294
  303.7 2.6 fusion.20
  306.3 2.6 fusion.18
  309.0 2.6 add_bitcast_fusion.2
  311.6 1.8 copy.135
  313.4 2.8 subtract_bitcast_fusion.2
  316.2 1.8 copy.138
  318.0 2.2 pad_maximum_fusion.3
  320.3 1.6 copy.139
  321.9 57.9 %all_to_all.22 = f32[2,3,2,384,256]{4,2,1,0,3:T(2,128)S(1)} all-to-all(f32[2,3,2,384,256]{4,2,1,0,3:T(2,128)S(1)} %copy.139), channel_id=1, replica_groups=mesh['grp'=4,'blk'=8,'ch'=4] {'grp','blk'}, dimensions={3} | all-to-all | bytes 9437184 | tf_op jit(solution)/shard_map/all_to_all | solution.py:79
  379.8 1.6 fusion.293
  381.4 0.2 copy.224
  381.6 0.2 copy.225
  381.9 0.2 fusion.67
  382.1 0.8 fusion.73
  383.1 1.1 fusion.72
  384.2 78.7 %psum.7 = f32[256]{0:T(256)S(1)} all-reduce(f32[256]{0:T(256)S(1)} %get-tuple-element.32), channel_id=1, replica_groups=mesh['grp'=4,'blk'=8,'ch'=4] {'grp','blk'}, use_global_device_ids=true, to_apply=%region_1.2 | all-reduce | flops 256 | bytes 2048 | tf_op jit(solution)/shard_map/psum | solution.py:141
  462.9 0.6 broadcast_multiply_fusion.1
  (21 shorter events, 0.9 us)
Async XLA Ops:
  0.6 2.3 copy-start
  96.6 75.8 %all-to-all-start.1 = ((f32[2,3,2,384,256]{4,2,1,0,3:T(2,128)}), f32[2,3,2,384,256]{4,2,1,0,3:T(2,128)}, u32[]{:S(2)}, u32[]{:S(2)}) async-start(f32[2,3,2,384,256]{4,2,1,0,3:T(2,128)} %copy.112), calls=%async_computation.1 | async-start | bytes 9437184 | tf_op jit(solution)/shard_map/all_to_all | solution.py:79
  381.8 1.1 copy-start.1
  381.9 1.1 copy-start.2
  381.9 1.1 copy-start.3
  381.9 1.2 copy-start.4
  381.9 1.2 copy-start.5
where the time goes:
time: 468 us; the launch traced here: 464 us
  blocking collectives  262 us (56%)
  matrix products  78.6 us (17%)
  waiting for transfers between devices  69.9 us (15%)
  local copies, waits for them, and re-layouts  32.8 us (7%)
  other arithmetic  13.8 us (3%)
  starting transfers between devices  5.26 us (1%)
    all_to_all x2, blocking collectives, across_whole(): lax.all_to_all(stacked, ('grp', 'blk'), split_axis=3, concat_axis=3, tile...  125 us
    psum x1, blocking collectives, body(): lax.psum(jnp.sum(upstream * mixed, axis=0), ('grp', 'blk')) * scale  78.7 us
    dot_general x24, matrix products, contract(): return jnp.einsum(form, values, table, precision=HIGHEST)  78.6 us
    all_to_all x1, waiting for transfers between devices, across_whole(): lax.all_to_all(joined, ('grp', 'blk'), split_axis=3, concat_axis=3, tiled...  69.9 us
    all_to_all x1, blocking collectives, across_whole(): lax.all_to_all(joined, ('grp', 'blk'), split_axis=3, concat_axis=3, tiled...  57.9 us
  transfers between devices with their start and end apart: 1, of which 1 were waited for; matrix products, arithmetic and copies ran while one was open for 0% of the time, Pallas kernels for 0%

commit v1 on v0

v1 whole, which is shorter than its diff:
```python
import math

import jax
import jax.numpy as jnp
import numpy as np
from jax import lax
from jax.experimental import pallas as pl
from jax.experimental.pallas import tpu as pltpu
from jax.sharding import PartitionSpec as P

AXES = ("grp", "blk")
LANES = 128
SUB = 8
INTERPRET = False


def split_table(table):
    high = table.astype(jnp.bfloat16)
    low = (table - high.astype(np.float64)).astype(jnp.bfloat16)
    return np.stack([high, low])


def tables(blocks, radix):
    total = blocks * radix * LANES
    eye = np.eye(SUB)
    near = np.arange(blocks)
    outer = 2.0 * np.pi * np.outer(near + 0.25, near) / blocks
    parts = np.stack([np.cos(outer), -np.sin(outer)])
    ahead = np.einsum("pkd,ce->pckde", parts, eye).reshape(2 * SUB * blocks, blocks * SUB)
    behind = ahead.T / total
    lane = np.arange(LANES)
    inner = 2.0 * np.pi * np.outer(lane, lane) / LANES
    cosine, sine = np.cos(inner), np.sin(inner)
    lane_ahead = np.block([[cosine, -sine], [sine, cosine]])
    lane_behind = np.block([[cosine, sine], [-sine, cosine]])
    piece = np.arange(radix)
    turn = 2.0 * np.pi * piece[:, None] * (near[None, :] + 0.25) / (blocks * radix)
    turn = np.broadcast_to(turn[:, :, None], (radix, blocks, LANES))
    key = near[None, :] + blocks * piece[:, None] + 0.25
    fine = 2.0 * np.pi * key[:, :, None] * lane[None, None, :] / total
    angles = np.stack([turn, fine])
    twist = np.stack([np.cos(angles), np.sin(angles)], axis=1).astype(np.float32)
    return (
        split_table(ahead),
        split_table(lane_ahead),
        split_table(lane_behind),
        split_table(behind),
        twist,
    )


def halves(values):
    high = values.astype(jnp.bfloat16)
    low = (values - high.astype(jnp.float32)).astype(jnp.bfloat16)
    return high, low


def dot(a, b):
    return jnp.dot(a, b, preferred_element_type=jnp.float32)


def pack_kernel(gate_in, value_in, gate_out, cotangent, taps, out):
    signals = (
        gate_in[...].astype(jnp.float32) * value_in[...].astype(jnp.float32),
        taps[...],
        cotangent[...].astype(jnp.float32) * gate_out[...].astype(jnp.float32),
    )
    radix = signals[0].shape[0] // LANES
    for s, signal in enumerate(signals):
        for a in range(radix):
            turned = signal[a * LANES : (a + 1) * LANES].T
            at = (a * 3 + s) * SUB
            out[:, at : at + SUB, :] = turned.reshape(-1, SUB, LANES)


def spectral_kernel(
    data, ahead, lane_ahead, lane_behind, behind, twist, out, xs, fs, gs, spec, gain
):
    blocks = data.shape[0]
    radix = twist.shape[2]
    half_root = math.sqrt(0.75)
    width = radix * LANES
    total = jnp.zeros((SUB, LANES), jnp.float32)
    for s in range(3):
        for a in range(radix):
            at = (a * 3 + s) * SUB
            high, low = halves(data[:, at : at + SUB, :].reshape(blocks * SUB, LANES))
            to = s * width + a * LANES
            xs[0, :, to : to + LANES] = high
            xs[1, :, to : to + LANES] = low
    for a in range(radix):
        mixed = data[:, a * 3 * SUB : a * 3 * SUB + SUB, :]
        up = data[:, (a * 3 + 2) * SUB : (a * 3 + 3) * SUB, :]
        total = total + jnp.sum(mixed * up, axis=0)
    skip_at = 3 * radix * SUB
    out[:, skip_at : skip_at + SUB, :] = jnp.broadcast_to(total[None], (blocks, SUB, LANES))

    first = dot(ahead[0], xs[0]) + dot(ahead[0], xs[1]) + dot(ahead[1], xs[0])
    fs[...] = first.reshape(2, SUB, blocks, 3 * width)

    for s in range(3):

        def forward(c, _, s=s):
            real, imag = [], []
            for a in range(radix):
                at = s * width + a * LANES
                re = fs[0, c, :, at : at + LANES]
                im = fs[1, c, :, at : at + LANES]
                if a:
                    co = twist[0, 0, a]
                    si = twist[0, 1, a]
                    re, im = re * co + im * si, im * co - re * si
                real.append(re)
                imag.append(im)
            sum_re, sum_im = real[1] + real[2], imag[1] + imag[2]
            mid_re, mid_im = real[0] - 0.5 * sum_re, imag[0] - 0.5 * sum_im
            dif_re = half_root * (real[1] - real[2])
            dif_im = half_root * (imag[1] - imag[2])
            outs = (
                (real[0] + sum_re, imag[0] + sum_im),
                (mid_re + dif_im, mid_im - dif_re),
                (mid_re - dif_im, mid_im + dif_re),
            )
            for e, (re, im) in enumerate(outs):
                co = twist[1, 0, e]
                si = twist[1, 1, e]
                for p, v in enumerate((re * co + im * si, im * co - re * si)):
                    high, low = halves(v)
                    gs[0, s, e, c, :, p * LANES : (p + 1) * LANES] = high
                    gs[1, s, e, c, :, p * LANES : (p + 1) * LANES] = low
            return 0

        lax.fori_loop(0, SUB, forward, 0)
        rows = radix * SUB * blocks
        high = gs[0, s].reshape(rows, 2 * LANES)
        low = gs[1, s].reshape(rows, 2 * LANES)
        result = dot(high, lane_ahead[0]) + dot(low, lane_ahead[0]) + dot(high, lane_ahead[1])
        spec[s] = result.reshape(radix, SUB, blocks, 2 * LANES)

    def product(c, _):
        for e in range(radix):
            mr, mi = spec[0, e, c, :, :LANES], spec[0, e, c, :, LANES:]
            hr, hi = spec[1, e, c, :, :LANES], spec[1, e, c, :, LANES:]
            ur, ui = spec[2, e, c, :, :LANES], spec[2, e, c, :, LANES:]
            outs = (
                (hr * mr - hi * mi, hr * mi + hi * mr),
                (hr * ur + hi * ui, hr * ui - hi * ur),
                (mr * ur + mi * ui, mr * ui - mi * ur),
            )
            for s, pair in enumerate(outs):
                for p, v in enumerate(pair):
                    high, low = halves(v)
                    gs[0, s, e, c, :, p * LANES : (p + 1) * LANES] = high
                    gs[1, s, e, c, :, p * LANES : (p + 1) * LANES] = low
        return 0

    lax.fori_loop(0, SUB, product, 0)

    for s in range(3):
        rows = radix * SUB * blocks
        high = gs[0, s].reshape(rows, 2 * LANES)
        low = gs[1, s].reshape(rows, 2 * LANES)
        result = dot(high, lane_behind[0]) + dot(low, lane_behind[0]) + dot(high, lane_behind[1])
        spec[s] = result.reshape(radix, SUB, blocks, 2 * LANES)

        def backward(c, _, s=s):
            real, imag = [], []
            for e in range(radix):
                re, im = spec[s, e, c, :, :LANES], spec[s, e, c, :, LANES:]
                co = twist[1, 0, e]
                si = twist[1, 1, e]
                real.append(re * co - im * si)
                imag.append(im * co + re * si)
            sum_re, sum_im = real[1] + real[2], imag[1] + imag[2]
            mid_re, mid_im = real[0] - 0.5 * sum_re, imag[0] - 0.5 * sum_im
            dif_re = half_root * (real[1] - real[2])
            dif_im = half_root * (imag[1] - imag[2])
            outs = (
                (real[0] + sum_re, imag[0] + sum_im),
                (mid_re - dif_im, mid_im + dif_re),
                (mid_re + dif_im, mid_im - dif_re),
            )
            for a, (re, im) in enumerate(outs):
                if a:
                    co = twist[0, 0, a]
                    si = twist[0, 1, a]
                    re, im = re * co - im * si, im * co + re * si
                at = s * width + a * LANES
                for p, v in enumerate((re, im)):
                    high, low = halves(v)
                    gain[0, p, c, :, at : at + LANES] = high
                    gain[1, p, c, :, at : at + LANES] = low
            return 0

        lax.fori_loop(0, SUB, backward, 0)

    rows = 2 * SUB * blocks
    high = gain[0].reshape(rows, 3 * width)
    low = gain[1].reshape(rows, 3 * width)
    result = dot(behind[0], high) + dot(behind[0], low) + dot(behind[1], high)
    for s in range(3):
        for a in range(radix):
            at = (a * 3 + s) * SUB
            to = s * width + a * LANES
            out[:, at : at + SUB, :] = result[:, to : to + LANES].reshape(blocks, SUB, LANES)


def unpack_kernel(
    data, gate_in, value_in, gate_out, cotangent, skip_gain, g_in, g_value, g_out, g_taps, g_skip, *, scale
):
    channels = gate_in.shape[1]
    radix = gate_in.shape[0] // LANES
    gain = skip_gain[...]
    for a in range(radix):
        rows = slice(a * LANES, (a + 1) * LANES)
        conv, back, lagged = (
            data[:, (a * 3 + s) * SUB : (a * 3 + s + 1) * SUB, :].reshape(channels, LANES).T
            for s in range(3)
        )
        first = gate_in[rows, :].astype(jnp.float32)
        value = value_in[rows, :].astype(jnp.float32)
        second = gate_out[rows, :].astype(jnp.float32)
        grad = cotangent[rows, :].astype(jnp.float32)
        g_out[rows, :] = (grad * (conv + gain * (first * value))).astype(g_out.dtype)
        mid = back + gain * (grad * second)
        g_in[rows, :] = (mid * value).astype(g_in.dtype)
        g_value[rows, :] = (mid * first).astype(g_value.dtype)
        g_taps[rows, :] = lagged * scale
    at = 3 * radix * SUB
    share = data[:, at : at + SUB, :].reshape(channels, LANES).T
    g_skip[...] = jnp.sum(share, axis=0, keepdims=True) * scale


PARAMS = pltpu.CompilerParams(vmem_limit_bytes=56 * 1024 * 1024)


def call(kernel, out_shape, scratch=()):
    return pl.pallas_call(
        kernel, out_shape=out_shape, scratch_shapes=scratch, compiler_params=PARAMS, interpret=INTERPRET
    )


def pack(gate_in, value_in, gate_out, cotangent, taps):
    rows, channels = taps.shape
    height = 3 * rows // LANES * SUB
    shape = jax.ShapeDtypeStruct((channels // SUB, height, LANES), jnp.float32)
    return call(pack_kernel, shape)(gate_in, value_in, gate_out, cotangent, taps)


def spectral(data):
    blocks = data.shape[0]
    radix = data.shape[1] // (3 * SUB)
    width = radix * LANES
    consts = [jnp.asarray(t) for t in tables(blocks, radix)]
    shape = jax.ShapeDtypeStruct((blocks, (3 * radix + 1) * SUB, LANES), jnp.float32)
    scratch = [
        pltpu.VMEM((2, blocks * SUB, 3 * width), jnp.bfloat16),
        pltpu.VMEM((2, SUB, blocks, 3 * width), jnp.float32),
        pltpu.VMEM((2, 3, radix, SUB, blocks, 2 * LANES), jnp.bfloat16),
        pltpu.VMEM((3, radix, SUB, blocks, 2 * LANES), jnp.float32),
        pltpu.VMEM((2, 2, SUB, blocks, 3 * width), jnp.bfloat16),
    ]
    return call(spectral_kernel, shape, scratch)(data, *consts)


def unpack(data, gate_in, value_in, gate_out, cotangent, skip_gain, scale):
    rows, channels = gate_in.shape
    half = jax.ShapeDtypeStruct((rows, channels), jnp.bfloat16)
    shapes = (
        half,
        half,
        half,
        jax.ShapeDtypeStruct((rows, channels), jnp.float32),
        jax.ShapeDtypeStruct((1, channels), jnp.float32),
    )

    def kernel(*refs):
        unpack_kernel(*refs, scale=scale)

    outs = call(kernel, shapes)(data, gate_in, value_in, gate_out, cotangent, skip_gain[None])
    return (*outs[:4], outs[4][0])


def body(gate_in, value_in, gate_out, filter_taps, skip_gain, cotangent):
    scale = 1.0 / math.sqrt(lax.axis_size(AXES) * gate_in.shape[0])
    data = pack(gate_in, value_in, gate_out, cotangent, filter_taps)
    data = lax.all_to_all(data, AXES, split_axis=0, concat_axis=0, tiled=True)
    data = spectral(data)
    data = lax.all_to_all(data, AXES, split_axis=0, concat_axis=0, tiled=True)
    return unpack(data, gate_in, value_in, gate_out, cotangent, skip_gain, scale)


def solution(mesh):
    spread = P(AXES, "ch")
    return jax.shard_map(
        body,
        mesh=mesh,
        in_specs=(spread, spread, spread, spread, P("ch"), spread),
        out_specs=(spread, spread, spread, spread, P("ch")),
        check_vma=False,
    )
```

time: 468 us -> 73 us (0.16)
  blocking collectives: 262 us -> 53 us
  matrix products: 78.6 us -> 0 us
  waiting for transfers between devices: 69.9 us -> 0 us
  local copies, waits for them, and re-layouts: 32.8 us -> 0 us
  Pallas kernels: 0 us -> 19 us
  other arithmetic: 13.8 us -> 0 us
  starting transfers between devices: 5.26 us -> 0 us
    all_to_all x3 -> x2, blocking collectives: 183 us -> 53 us  [body(): data = lax.all_to_all(data, AXES, split_axis=0, concat_axis=0, tiled=True)]
    psum x1 -> x0, blocking collectives: 78.7 us -> none  [body(): lax.psum(jnp.sum(upstream * mixed, axis=0), ('grp', 'blk')) * scale]
    dot_general x24 -> x0, matrix products: 78.6 us -> none  [contract(): return jnp.einsum(form, values, table, precision=HIGHEST)]
    all_to_all x1 -> x0, waiting for transfers between devices: 69.9 us -> none  [across_whole(): lax.all_to_all(joined, ('grp', 'blk'), split_axis=3, concat_axis=3, tiled...]
    pallas_call x0 -> x3, Pallas kernels: none -> 19 us  [the longest x1 13.4 us: spectral(): return call(spectral_kernel, shape, scratch)(data, *consts)]
    another operation x4 -> x0, local copies, waits for them, and re-layouts: 12.7 us -> none  [the longest x2 7.28 us: body(): stacked = jnp.stack([real_part, imag_part])]
    slice x4 -> x0, local copies, waits for them, and re-layouts: 8.9 us -> none  [the longest x1 4.04 us: body(): real_part, imag_part = twist(stacked[0], stacked[1], theta, 1.0)]
    another operation x8 -> x0, other arithmetic: 8.04 us -> none  [the longest x2 4.45 us: across_whole(): joined = jnp.stack([real_part, imag_part]).reshape(shape)]
  transfers between devices with their start and end apart: 1 -> 0, of which waited for: 1 -> 0; matrix products, arithmetic and copies ran while one was open for 0% -> 0% of each run, Pallas kernels for 0% -> 0%
where the time goes in v1:
time: 73 us; the launch traced here: 72.6 us
  blocking collectives  53 us (73%)
  Pallas kernels  19 us (26%)
    all_to_all x2, blocking collectives, body(): data = lax.all_to_all(data, AXES, split_axis=0, concat_axis=0, tiled=True)  53 us
    pallas_call x1, Pallas kernels, spectral(): return call(spectral_kernel, shape, scratch)(data, *consts)  13.4 us
    pallas_call x1, Pallas kernels, unpack(): call(kernel, shapes)  2.87 us
    pallas_call x1, Pallas kernels, pack(): call(pack_kernel, shape)(gate_in, value_in, gate_out, cotangent, taps)  2.74 us

profile of v1, /device:TPU:0, one launch (start us, length us, event | category | flops | bytes accessed | tf_op | source)
XLA Modules:
  0.0 72.6 jit_solution(7438912119486323983)
XLA Ops:
  0.6 2.7 %shard_map.146 = f32[32,72,128]{2,1,0:T(8,128)} custom-call(bf16[384,256]{1,0:T(8,128)(2,1)} %refs_1_.1, bf16[384,256]{1,0:T(8,128)(2,1)} %refs_2_.1, bf16[384,256]{1,0:T(8,128)(2,1)} %refs_3_.1, bf16[384,256]{1,0:T(8,128)(2,1)} %refs_4_.1, f32[384,256]{1,0:T(8,128)} %taps.1), custom_call_target="tpu_custom_call" | custom-call | tf_op jit(solution)/shard_map/pallas_call | solution.py:247
  3.4 28.7 %all_to_all.10.data = f32[32,72,128]{2,1,0:T(8,128)} all-to-all(f32[32,72,128]{2,1,0:T(8,128)} %shard_map.146), channel_id=1, replica_groups=mesh['grp'=4,'blk'=8,'ch'=4] {'grp','blk'}, dimensions={0} | all-to-all | bytes 2359296 | tf_op jit(solution)/shard_map/all_to_all | solution.py:287
  32.1 13.4 %shard_map.147 = f32[32,80,128]{2,1,0:T(8,128)} custom-call(f32[32,72,128]{2,1,0:T(8,128)} %all_to_all.10.data, bf16[2,512,256]{2,1,0:T(8,128)(2,1)} %constant.10.clone.ahead, bf16[2,256,256]{2,1,0:T(8,128)(2,1)} %constant.11.clone.lane_ahead, bf16[2,256,256]{2,1,0:T(8,128)(2,1)} %constant.12.clone.lane_behind, bf16[2,256,512]{2,1,0:T(8,128)(2,1)} %constant.13.clone.behind, ...), custom_call_target="tpu_custom_call" | custom-call | tf_op jit(solution)/shard_map/pallas_call | solution.py:263
  45.5 24.2 %all_to_all.11.refs_0_ = f32[32,80,128]{2,1,0:T(8,128)} all-to-all(f32[32,80,128]{2,1,0:T(8,128)} %shard_map.147), channel_id=1, replica_groups=mesh['grp'=4,'blk'=8,'ch'=4] {'grp','blk'}, dimensions={0} | all-to-all | bytes 2621440 | tf_op jit(solution)/shard_map/all_to_all | solution.py:289
  69.7 2.9 %shard_map.148 = (bf16[384,256]{1,0:T(8,128)(2,1)}, bf16[384,256]{1,0:T(8,128)(2,1)}, bf16[384,256]{1,0:T(8,128)(2,1)}, f32[384,256]{1,0:T(8,128)}, f32[1,256]{1,0:T(1,128)}) custom-call(f32[32,80,128]{2,1,0:T(8,128)} %all_to_all.11.refs_0_, bf16[384,256]{1,0:T(8,128)(2,1)} %refs_1_.1, bf16[384,256]{1,0:T(8,128)(2,1)} %refs_2_.1, bf16[384,256]{1,0:T(8,128)(2,1)} %refs_3_.1, ...), custom_call_target="tpu_custom_call" | custom-call | tf_op jit(solution)/shard_map/pallas_call | solution.py:280

commit v2 on v1

--- a/solution.py
+++ b/solution.py
@@ -14,10 +14,10 @@
 INTERPRET = False
 
 
-def split_table(table):
+def split_table(table, axis):
     high = table.astype(jnp.bfloat16)
     low = (table - high.astype(np.float64)).astype(jnp.bfloat16)
-    return np.stack([high, low])
+    return np.concatenate([high, high, low], axis=axis)
 
 
 def tables(blocks, radix):
@@ -41,10 +41,10 @@
     angles = np.stack([turn, fine])
     twist = np.stack([np.cos(angles), np.sin(angles)], axis=1).astype(np.float32)
     return (
-        split_table(ahead),
-        split_table(lane_ahead),
-        split_table(lane_behind),
-        split_table(behind),
+        split_table(ahead, 1),
+        split_table(lane_ahead, 0),
+        split_table(lane_behind, 0),
+        split_table(behind, 1),
         twist,
     )
 
@@ -59,18 +59,29 @@
     return jnp.dot(a, b, preferred_element_type=jnp.float32)
 
 
-def pack_kernel(gate_in, value_in, gate_out, cotangent, taps, out):
-    signals = (
-        gate_in[...].astype(jnp.float32) * value_in[...].astype(jnp.float32),
-        taps[...],
-        cotangent[...].astype(jnp.float32) * gate_out[...].astype(jnp.float32),
-    )
-    radix = signals[0].shape[0] // LANES
-    for s, signal in enumerate(signals):
+def pack_kernel(taps_in, gate_in, value_in, cotangent_in, gate_out_in, out, *scratch):
+    sources = (taps_in, gate_in, value_in, cotangent_in, gate_out_in)
+    buffers, sems = scratch[:5], scratch[5]
+    copies = [pltpu.make_async_copy(src, dst, sems.at[i]) for i, (src, dst) in enumerate(zip(sources, buffers))]
+    for copy in copies:
+        copy.start()
+    radix = taps_in.shape[0] // LANES
+    taps, first, value, grad, second = buffers
+
+    def send(s, take):
         for a in range(radix):
-            turned = signal[a * LANES : (a + 1) * LANES].T
+            turned = take(slice(a * LANES, (a + 1) * LANES)).T
             at = (a * 3 + s) * SUB
             out[:, at : at + SUB, :] = turned.reshape(-1, SUB, LANES)
+
+    copies[0].wait()
+    send(1, lambda r: taps[r, :])
+    copies[1].wait()
+    copies[2].wait()
+    send(0, lambda r: first[r, :].astype(jnp.float32) * value[r, :].astype(jnp.float32))
+    copies[3].wait()
+    copies[4].wait()
+    send(2, lambda r: grad[r, :].astype(jnp.float32) * second[r, :].astype(jnp.float32))
 
 
 def spectral_kernel(
@@ -86,8 +97,8 @@
             at = (a * 3 + s) * SUB
             high, low = halves(data[:, at : at + SUB, :].reshape(blocks * SUB, LANES))
             to = s * width + a * LANES
-            xs[0, :, to : to + LANES] = high
-            xs[1, :, to : to + LANES] = low
+            for j, v in enumerate((high, low, high)):
+                xs[j, :, to : to + LANES] = v
     for a in range(radix):
         mixed = data[:, a * 3 * SUB : a * 3 * SUB + SUB, :]
         up = data[:, (a * 3 + 2) * SUB : (a * 3 + 3) * SUB, :]
@@ -95,8 +106,8 @@
     skip_at = 3 * radix * SUB
     out[:, skip_at : skip_at + SUB, :] = jnp.broadcast_to(total[None], (blocks, SUB, LANES))
 
-    first = dot(ahead[0], xs[0]) + dot(ahead[0], xs[1]) + dot(ahead[1], xs[0])
-    fs[...] = first.reshape(2, SUB, blocks, 3 * width)
+    stacked = xs[...].reshape(3 * blocks * SUB, 3 * width)
+    fs[...] = dot(ahead[...], stacked).reshape(2, SUB, blocks, 3 * width)
 
     for s in range(3):
 
@@ -126,15 +137,14 @@
                 si = twist[1, 1, e]
                 for p, v in enumerate((re * co + im * si, im * co - re * si)):
                     high, low = halves(v)
-                    gs[0, s, e, c, :, p * LANES : (p + 1) * LANES] = high
-                    gs[1, s, e, c, :, p * LANES : (p + 1) * LANES] = low
+                    for j, w in enumerate((high, low, high)):
+                        at = (2 * j + p) * LANES
+                        gs[s, e, c, :, at : at + LANES] = w
             return 0
 
-        lax.fori_loop(0, SUB, forward, 0)
+        lax.fori_loop(0, SUB, forward, 0, unroll=True)
         rows = radix * SUB * blocks
-        high = gs[0, s].reshape(rows, 2 * LANES)
-        low = gs[1, s].reshape(rows, 2 * LANES)
-        result = dot(high, lane_ahead[0]) + dot(low, lane_ahead[0]) + dot(high, lane_ahead[1])
+        result = dot(gs[s].reshape(rows, 6 * LANES), lane_ahead[...])
         spec[s] = result.reshape(radix, SUB, blocks, 2 * LANES)
 
     def product(c, _):
@@ -150,17 +160,16 @@
             for s, pair in enumerate(outs):
                 for p, v in enumerate(pair):
                     high, low = halves(v)
-                    gs[0, s, e, c, :, p * LANES : (p + 1) * LANES] = high
-                    gs[1, s, e, c, :, p * LANES : (p + 1) * LANES] = low
+                    for j, w in enumerate((high, low, high)):
+                        at = (2 * j + p) * LANES
+                        gs[s, e, c, :, at : at + LANES] = w
         return 0
 
-    lax.fori_loop(0, SUB, product, 0)
+    lax.fori_loop(0, SUB, product, 0, unroll=True)
 
     for s in range(3):
         rows = radix * SUB * blocks
-        high = gs[0, s].reshape(rows, 2 * LANES)
-        low = gs[1, s].reshape(rows, 2 * LANES)
-        result = dot(high, lane_behind[0]) + dot(low, lane_behind[0]) + dot(high, lane_behind[1])
+        result = dot(gs[s].reshape(rows, 6 * LANES), lane_behind[...])
         spec[s] = result.reshape(radix, SUB, blocks, 2 * LANES)
 
         def backward(c, _, s=s):
@@ -188,16 +197,14 @@
                 at = s * width + a * LANES
                 for p, v in enumerate((re, im)):
                     high, low = halves(v)
-                    gain[0, p, c, :, at : at + LANES] = high
-                    gain[1, p, c, :, at : at + LANES] = low
+                    for j, w in enumerate((high, low, high)):
+                        gain[j, p, c, :, at : at + LANES] = w
             return 0
 
-        lax.fori_loop(0, SUB, backward, 0)
-
-    rows = 2 * SUB * blocks
-    high = gain[0].reshape(rows, 3 * width)
-    low = gain[1].reshape(rows, 3 * width)
-    result = dot(behind[0], high) + dot(behind[0], low) + dot(behind[1], high)
+        lax.fori_loop(0, SUB, backward, 0, unroll=True)
+
+    stacked = gain[...].reshape(3 * 2 * SUB * blocks, 3 * width)
+    result = dot(behind[...], stacked)
     for s in range(3):
         for a in range(radix):
             at = (a * 3 + s) * SUB
@@ -231,12 +238,26 @@
     g_skip[...] = jnp.sum(share, axis=0, keepdims=True) * scale
 
 
-PARAMS = pltpu.CompilerParams(vmem_limit_bytes=56 * 1024 * 1024)
-
-
-def call(kernel, out_shape, scratch=()):
+PARAMS = pltpu.CompilerParams(vmem_limit_bytes=24 * 1024 * 1024)
+ON_CHIP = pl.BlockSpec(memory_space=pltpu.VMEM)
+IN_HBM = pl.BlockSpec(memory_space=pltpu.HBM)
+
+
+def held(x):
+    return x if INTERPRET else pltpu.with_memory_space_constraint(x, pltpu.HBM)
+
+
+def call(kernel, out_shape, scratch=(), in_specs=None):
+    extra = {} if in_specs is None else {"in_specs": in_specs}
+    out_specs = jax.tree.map(lambda _: ON_CHIP, out_shape)
     return pl.pallas_call(
-        kernel, out_shape=out_shape, scratch_shapes=scratch, compiler_params=PARAMS, interpret=INTERPRET
+        kernel,
+        out_shape=out_shape,
+        out_specs=out_specs,
+        scratch_shapes=scratch,
+        compiler_params=PARAMS,
+        interpret=INTERPRET,
+        **extra,
     )
 
 
@@ -244,7 +265,10 @@
     rows, channels = taps.shape
     height = 3 * rows // LANES * SUB
     shape = jax.ShapeDtypeStruct((channels // SUB, height, LANES), jnp.float32)
-    return call(pack_kernel, shape)(gate_in, value_in, gate_out, cotangent, taps)
+    operands = tuple(held(x) for x in (taps, gate_in, value_in, cotangent, gate_out))
+    scratch = [pltpu.VMEM(x.shape, x.dtype) for x in operands]
+    scratch.append(pltpu.SemaphoreType.DMA((len(operands),)))
+    return call(pack_kernel, shape, scratch, [IN_HBM] * len(operands))(*operands)
 
 
 def spectral(data):
@@ -254,11 +278,11 @@
     consts = [jnp.asarray(t) for t in tables(blocks, radix)]
     shape = jax.ShapeDtypeStruct((blocks, (3 * radix + 1) * SUB, LANES), jnp.float32)
     scratch = [
-        pltpu.VMEM((2, blocks * SUB, 3 * width), jnp.bfloat16),
+        pltpu.VMEM((3, blocks * SUB, 3 * width), jnp.bfloat16),
         pltpu.VMEM((2, SUB, blocks, 3 * width), jnp.float32),
-        pltpu.VMEM((2, 3, radix, SUB, blocks, 2 * LANES), jnp.bfloat16),
+        pltpu.VMEM((3, radix, SUB, blocks, 6 * LANES), jnp.bfloat16),
         pltpu.VMEM((3, radix, SUB, blocks, 2 * LANES), jnp.float32),
-        pltpu.VMEM((2, 2, SUB, blocks, 3 * width), jnp.bfloat16),
+        pltpu.VMEM((3, 2, SUB, blocks, 3 * width), jnp.bfloat16),
     ]
     return call(spectral_kernel, shape, scratch)(data, *consts)
 

time: 73 us -> 61.5 us (0.84)
  Pallas kernels: 19 us -> 8.69 us
  blocking collectives: 53 us -> 51.8 us
    pallas_call x1, Pallas kernels: 13.4 us -> 5.8 us  [spectral(): return call(spectral_kernel, shape, scratch)(data, *consts)]
    pallas_call x1, Pallas kernels: 2.87 us -> 1.3 us  [unpack(): call(kernel, shapes)]
    all_to_all x2, blocking collectives: 53 us -> 51.8 us  [body(): data = lax.all_to_all(data, AXES, split_axis=0, concat_axis=0, tiled=True)]
    pallas_call x1, Pallas kernels: 2.74 us -> 1.59 us  [pack(): call(pack_kernel, shape, scratch, [IN_HBM] * len(operands))(*operands)]
where the time goes in v2:
time: 61.5 us; the launch traced here: 61.3 us
  blocking collectives  51.8 us (84%)
  Pallas kernels  8.69 us (14%)
  between operations  0.76 us (1%)
    all_to_all x2, blocking collectives, body(): data = lax.all_to_all(data, AXES, split_axis=0, concat_axis=0, tiled=True)  51.8 us
    pallas_call x1, Pallas kernels, spectral(): return call(spectral_kernel, shape, scratch)(data, *consts)  5.8 us
    pallas_call x1, Pallas kernels, pack(): call(pack_kernel, shape, scratch, [IN_HBM] * len(operands))(*operands)  1.59 us
    pallas_call x1, Pallas kernels, unpack(): call(kernel, shapes)  1.3 us

profile of v2, /device:TPU:0, one launch (start us, length us, event | category | flops | bytes accessed | tf_op | source)
XLA Modules:
  0.0 61.3 jit_solution(5342902871753858764)
XLA Ops:
  0.6 0.0 copy-start.8
  0.6 1.6 %shard_map.146 = f32[32,72,128]{2,1,0:T(8,128)S(1)} custom-call(f32[384,256]{1,0:T(8,128)} %taps_in.1, bf16[384,256]{1,0:T(8,128)(2,1)} %refs_1_.1, bf16[384,256]{1,0:T(8,128)(2,1)} %refs_2_.1, bf16[384,256]{1,0:T(8,128)(2,1)} %refs_4_.1, bf16[384,256]{1,0:T(8,128)(2,1)} %refs_3_.1), custom_call_target="tpu_custom_call" | custom-call | tf_op jit(solution)/shard_map/pallas_call | solution.py:271
  2.2 0.0 copy-start
  2.3 0.0 copy-start.1
  2.3 0.0 copy-start.6
  2.3 0.0 copy-start.7
  2.3 28.6 %all_to_all.10.data = f32[32,72,128]{2,1,0:T(8,128)S(1)} all-to-all(f32[32,72,128]{2,1,0:T(8,128)S(1)} %shard_map.146), channel_id=1, replica_groups=mesh['grp'=4,'blk'=8,'ch'=4] {'grp','blk'}, dimensions={0} | all-to-all | bytes 2359296 | tf_op jit(solution)/shard_map/all_to_all | solution.py:311
  30.9 0.0 copy-done.8
  30.9 0.0 copy-done
  30.9 0.0 copy-done.1
  30.9 0.0 copy-done.6
  30.9 0.0 copy-done.7
  30.9 5.8 %shard_map.147 = f32[32,80,128]{2,1,0:T(8,128)S(1)} custom-call(f32[32,72,128]{2,1,0:T(8,128)S(1)} %all_to_all.10.data, bf16[512,768]{1,0:T(8,128)(2,1)S(1)} %copy-done.1, bf16[768,256]{1,0:T(8,128)(2,1)S(1)} %copy-done.7, bf16[768,256]{1,0:T(8,128)(2,1)S(1)} %copy-done.6, bf16[256,1536]{1,0:T(8,128)(2,1)S(1)} %copy-done, f32[2,2,3,32,128]{4,3,2,1,0:T(8,128)S(1)} %copy-done.8), custom_call_target="tpu_custom_call" | custom-call | tf_op jit(solution)/shard_map/pallas_call | solution.py:287
  36.7 0.0 copy-start.2
  36.7 0.0 copy-start.3
  36.7 0.0 copy-start.4
  36.7 0.0 copy-start.5
  36.7 0.0 copy-start.9
  36.7 23.2 %all_to_all.11.refs_0_ = f32[32,80,128]{2,1,0:T(8,128)S(1)} all-to-all(f32[32,80,128]{2,1,0:T(8,128)S(1)} %shard_map.147), channel_id=1, replica_groups=mesh['grp'=4,'blk'=8,'ch'=4] {'grp','blk'}, dimensions={0} | all-to-all | bytes 2621440 | tf_op jit(solution)/shard_map/all_to_all | solution.py:313
  60.0 0.0 copy-done.2
  60.0 0.0 copy-done.3
  60.0 0.0 copy-done.4
  60.0 0.0 copy-done.5
  60.0 0.0 copy-done.9
  60.0 1.3 %shard_map.148 = (bf16[384,256]{1,0:T(8,128)(2,1)}, bf16[384,256]{1,0:T(8,128)(2,1)}, bf16[384,256]{1,0:T(8,128)(2,1)}, f32[384,256]{1,0:T(8,128)}, f32[1,256]{1,0:T(1,128)}) custom-call(f32[32,80,128]{2,1,0:T(8,128)S(1)} %all_to_all.11.refs_0_, bf16[384,256]{1,0:T(8,128)(2,1)S(1)} %copy-done.2, bf16[384,256]{1,0:T(8,128)(2,1)S(1)} %copy-done.3, ...), custom_call_target="tpu_custom_call" | custom-call | tf_op jit(solution)/shard_map/pallas_call | solution.py:304
Async XLA Ops:
  0.6 30.2 %copy-start.8 = (f32[2,2,3,32,128]{4,3,2,1,0:T(8,128)S(1)}, f32[2,2,3,32,128]{4,3,2,1,0:T(8,128)}, u32[]{:S(2)}) copy-start(f32[2,2,3,32,128]{4,3,2,1,0:T(8,128)} %constant.14.clone.twist) | copy-start | bytes 589828
  2.2 28.6 %copy-start = (bf16[256,1536]{1,0:T(8,128)(2,1)S(1)}, bf16[256,1536]{1,0:T(8,128)(2,1)}, u32[]{:S(2)}) copy-start(bf16[256,1536]{1,0:T(8,128)(2,1)} %constant.13.clone.behind) | copy-start | bytes 2359300
  2.3 28.6 %copy-start.1 = (bf16[512,768]{1,0:T(8,128)(2,1)S(1)}, bf16[512,768]{1,0:T(8,128)(2,1)}, u32[]{:S(2)}) copy-start(bf16[512,768]{1,0:T(8,128)(2,1)} %constant.10.clone.ahead) | copy-start | bytes 2359300
  2.3 28.6 %copy-start.6 = (bf16[768,256]{1,0:T(8,128)(2,1)S(1)}, bf16[768,256]{1,0:T(8,128)(2,1)}, u32[]{:S(2)}) copy-start(bf16[768,256]{1,0:T(8,128)(2,1)} %constant.12.clone.lane_behind) | copy-start | bytes 1179652
  2.3 28.6 %copy-start.7 = (bf16[768,256]{1,0:T(8,128)(2,1)S(1)}, bf16[768,256]{1,0:T(8,128)(2,1)}, u32[]{:S(2)}) copy-start(bf16[768,256]{1,0:T(8,128)(2,1)} %constant.11.clone.lane_ahead) | copy-start | bytes 1179652
  36.7 23.3 %copy-start.2 = (bf16[384,256]{1,0:T(8,128)(2,1)S(1)}, bf16[384,256]{1,0:T(8,128)(2,1)}, u32[]{:S(2)}) copy-start(bf16[384,256]{1,0:T(8,128)(2,1)} %refs_1_.1) | copy-start | bytes 589828
  36.7 23.3 %copy-start.3 = (bf16[384,256]{1,0:T(8,128)(2,1)S(1)}, bf16[384,256]{1,0:T(8,128)(2,1)}, u32[]{:S(2)}) copy-start(bf16[384,256]{1,0:T(8,128)(2,1)} %refs_2_.1) | copy-start | bytes 589828
  36.7 23.3 %copy-start.4 = (bf16[384,256]{1,0:T(8,128)(2,1)S(1)}, bf16[384,256]{1,0:T(8,128)(2,1)}, u32[]{:S(2)}) copy-start(bf16[384,256]{1,0:T(8,128)(2,1)} %refs_4_.1) | copy-start | bytes 589828
  36.7 23.3 %copy-start.5 = (bf16[384,256]{1,0:T(8,128)(2,1)S(1)}, bf16[384,256]{1,0:T(8,128)(2,1)}, u32[]{:S(2)}) copy-start(bf16[384,256]{1,0:T(8,128)(2,1)} %refs_3_.1) | copy-start | bytes 589828
  36.7 23.3 %copy-start.9 = (f32[256]{0:T(256)S(1)}, f32[256]{0:T(256)}, u32[]{:S(2)}) copy-start(f32[256]{0:T(256)} %param.15) | copy-start | bytes 3076

commit v3 on v2

v3 whole, which is shorter than its diff:
```python
import math

import jax
import jax.numpy as jnp
import numpy as np
from jax import lax
from jax.experimental import pallas as pl
from jax.experimental.pallas import tpu as pltpu
from jax.sharding import PartitionSpec as P

AXES = ("grp", "blk")
LANES = 128
SUB = 8
INTERPRET = False


def split_table(table):
    high = table.astype(jnp.bfloat16)
    low = (table - high.astype(np.float64)).astype(jnp.bfloat16)
    return np.concatenate([high, high, low], axis=0)


NEAR, FAR = 4, 8


def tables(blocks, radix):
    total = blocks * radix * LANES
    lane = np.arange(LANES)
    inner = 2.0 * np.pi * np.outer(lane, lane) / LANES
    cosine, sine = np.cos(inner), np.sin(inner)
    lane_ahead = np.block([[cosine, -sine], [sine, cosine]])
    lane_behind = np.block([[cosine, sine], [-sine, cosine]])
    far, near, piece = np.meshgrid(np.arange(FAR), np.arange(NEAR), np.arange(radix), indexing="ij")
    span = blocks * radix
    from_piece = blocks * pow(blocks, -1, radix) * pow(radix - 1, -1, radix)
    from_block = radix * pow(radix, -1, blocks) * radix
    key = (from_piece * piece + from_block * (far + FAR * near)) % span
    fine = 2.0 * np.pi * (key.reshape(-1, 1) + 0.25) * lane / total
    twist = np.stack([np.cos(fine), np.sin(fine)]).astype(np.float32)
    twist = np.repeat(twist[:, :, None, :], SUB, axis=2)
    return split_table(lane_ahead), split_table(lane_behind), twist


def halves(values):
    high = values.astype(jnp.bfloat16)
    low = (values - high.astype(jnp.float32)).astype(jnp.bfloat16)
    return high, low


def dot(a, b):
    return jnp.dot(a, b, preferred_element_type=jnp.float32)


def turn(pair, angle):
    re, im = pair
    eighth = round(angle * 8) % 8
    if abs(angle * 8 - round(angle * 8)) < 1e-9:
        if eighth == 0:
            return re, im
        if eighth == 2:
            return -im, re
        if eighth == 4:
            return -re, -im
        if eighth == 6:
            return im, -re
        root = math.sqrt(0.5)
        if eighth == 1:
            return root * (re - im), root * (re + im)
        if eighth == 3:
            return -root * (re + im), root * (re - im)
        if eighth == 5:
            return root * (im - re), -root * (re + im)
        return root * (re + im), root * (im - re)
    c, s = math.cos(2.0 * math.pi * angle), math.sin(2.0 * math.pi * angle)
    return c * re - s * im, c * im + s * re


def plus(x, y):
    return x[0] + y[0], x[1] + y[1]


def minus(x, y):
    return x[0] - y[0], x[1] - y[1]


def plus_i(x, y, sign):
    if sign > 0:
        return x[0] - y[1], x[1] + y[0]
    return x[0] + y[1], x[1] - y[0]


def four(x, sign):
    p, m = plus(x[0], x[2]), minus(x[0], x[2])
    q, n = plus(x[1], x[3]), minus(x[1], x[3])
    return [plus(p, q), plus_i(m, n, sign), minus(p, q), plus_i(m, n, -sign)]


def eight(x, sign):
    even, odd = four(x[0::2], sign), four(x[1::2], sign)
    odd = [odd[0]] + [turn(odd[k], sign * k / 8) for k in (1, 2, 3)]
    return [plus(even[k], odd[k]) for k in range(4)] + [minus(even[k], odd[k]) for k in range(4)]


def three(x, sign):
    total, gap = plus(x[1], x[2]), minus(x[1], x[2])
    half_root = math.sqrt(0.75)
    mid = x[0][0] - 0.5 * total[0], x[0][1] - 0.5 * total[1]
    gap = half_root * gap[0], half_root * gap[1]
    return [plus(x[0], total), plus_i(mid, gap, sign), plus_i(mid, gap, -sign)]


def pack_kernel(taps_in, gate_in, value_in, cotangent_in, gate_out_in, out, *scratch):
    sources = (taps_in, gate_in, value_in, cotangent_in, gate_out_in)
    buffers, sems = scratch[:5], scratch[5]
    copies = [pltpu.make_async_copy(src, dst, sems.at[i]) for i, (src, dst) in enumerate(zip(sources, buffers))]
    for copy in copies:
        copy.start()
    radix = taps_in.shape[0] // LANES
    taps, first, value, grad, second = buffers

    def send(s, take):
        for a in range(radix):
            turned = take(slice(a * LANES, (a + 1) * LANES)).T
            at = (a * 3 + s) * SUB
            out[:, at : at + SUB, :] = turned.reshape(-1, SUB, LANES)

    copies[0].wait()
    send(1, lambda r: taps[r, :])
    copies[1].wait()
    copies[2].wait()
    send(0, lambda r: first[r, :].astype(jnp.float32) * value[r, :].astype(jnp.float32))
    copies[3].wait()
    copies[4].wait()
    send(2, lambda r: grad[r, :].astype(jnp.float32) * second[r, :].astype(jnp.float32))


def spectral_kernel(data, lane_ahead, lane_behind, twist, out, ts, gs, spec):
    blocks = data.shape[0]
    radix = data.shape[1] // (3 * SUB)
    span = blocks * radix
    scale = 1.0 / (span * LANES)
    height = 3 * radix * SUB + 1
    rows = span * SUB

    def at(a, s):
        return slice((a * 3 + s) * SUB, (a * 3 + s + 1) * SUB)

    total = jnp.zeros((SUB, LANES), jnp.float32)
    for a in range(radix):
        total = total + jnp.sum(data[:, at(a, 0), :] * data[:, at(a, 2), :], axis=0)
    share = jnp.concatenate([jnp.sum(total.T, axis=0, keepdims=True)] * (LANES // SUB), axis=1)
    for d in range(blocks):
        out[d * height + height - 1 : (d + 1) * height, :] = share

    def store(s, row, pairs):
        for p in range(2):
            high, low = halves(jnp.concatenate([pair[p] for pair in pairs], axis=0))
            for j, w in enumerate((high, low, high)):
                lanes = (2 * j + p) * LANES
                gs[s, row : row + 2 * SUB, lanes : lanes + LANES] = w

    def forward(s):
        for a in range(radix):
            for n0 in range(NEAR):
                values = []
                for n1 in range(FAR):
                    m = NEAR * n1 + n0
                    d = ((m - a) * pow(radix, -1, blocks)) % blocks
                    x = data[d, at(a, s), :]
                    angle = 2.0 * math.pi * (radix * d + a) / (4 * span)
                    values.append((math.cos(angle) * x, -math.sin(angle) * x))
                for k1, pair in enumerate(eight(values, -1)):
                    re, im = turn(pair, -n0 * k1 / blocks)
                    ts[s, a, n0, k1, 0] = re
                    ts[s, a, n0, k1, 1] = im
        for k1 in range(FAR):
            quads = [
                four([(ts[s, a, n0, k1, 0], ts[s, a, n0, k1, 1]) for n0 in range(NEAR)], -1)
                for a in range(radix)
            ]
            for k2 in range(0, NEAR, 2):
                pairs = []
                for k in (k2, k2 + 1):
                    group = []
                    for e, (re, im) in enumerate(three([quads[a][k] for a in range(radix)], -1)):
                        row = (k1 * NEAR + k) * radix + e
                        co, si = twist[0, row], twist[1, row]
                        group.append((re * co + im * si, im * co - re * si))
                    pairs.append(group)
                for e in range(radix):
                    row = (e * blocks + k1 * NEAR + k2) * SUB
                    store(s, row, [pairs[0][e], pairs[1][e]])
        spec[s] = dot(gs[s], lane_ahead[...])

    def product(s):
        left, right = ((1, 0), (1, 2), (0, 2))[s]
        for row in range(0, rows, 2 * SUB):
            lr, li = spec[left, row : row + 2 * SUB, :LANES], spec[left, row : row + 2 * SUB, LANES:]
            rr, ri = spec[right, row : row + 2 * SUB, :LANES], spec[right, row : row + 2 * SUB, LANES:]
            if s == 0:
                both = lr * rr - li * ri, lr * ri + li * rr
            else:
                both = lr * rr + li * ri, lr * ri - li * rr
            for p in range(2):
                high, low = halves(both[p])
                for j, w in enumerate((high, low, high)):
                    lanes = (2 * j + p) * LANES
                    gs[3 + s, row : row + 2 * SUB, lanes : lanes + LANES] = w
        spec[3 + s] = dot(gs[3 + s], lane_behind[...])

    def backward(s):
        for k1 in range(FAR):
            quads = []
            for k2 in range(NEAR):
                trio = []
                for e in range(radix):
                    row = (e * blocks + k1 * NEAR + k2) * SUB
                    re, im = spec[3 + s, row : row + SUB, :LANES], spec[3 + s, row : row + SUB, LANES:]
                    row = (k1 * NEAR + k2) * radix + e
                    co, si = twist[0, row], twist[1, row]
                    trio.append((re * co - im * si, im * co + re * si))
                quads.append(three(trio, 1))
            for a in range(radix):
                for n0, pair in enumerate(four([quads[k2][a] for k2 in range(NEAR)], 1)):
                    re, im = turn(pair, n0 * k1 / blocks)
                    ts[s, a, n0, k1, 0] = re
                    ts[s, a, n0, k1, 1] = im
        for a in range(radix):
            for n0 in range(NEAR):
                values = eight([(ts[s, a, n0, k1, 0], ts[s, a, n0, k1, 1]) for k1 in range(FAR)], 1)
                for n1, (re, im) in enumerate(values):
                    m = NEAR * n1 + n0
                    d = ((m - a) * pow(radix, -1, blocks)) % blocks
                    angle = 2.0 * math.pi * (radix * d + a) / (4 * span)
                    row = d * height + (a * 3 + s) * SUB
                    out[row : row + SUB, :] = (scale * math.cos(angle)) * re - (scale * math.sin(angle)) * im

    forward(0)
    forward(1)
    product(0)
    forward(2)
    backward(0)
    product(1)
    product(2)
    backward(1)
    backward(2)


def unpack_kernel(
    data, gate_in, value_in, gate_out, cotangent, skip_gain, g_in, g_value, g_out, g_taps, g_skip, *, scale
):
    channels = gate_in.shape[1]
    radix = gate_in.shape[0] // LANES
    gain = skip_gain[...]
    height = 3 * radix * SUB + 1

    def piece(a, s):
        at = (a * 3 + s) * SUB
        tiles = [data[d * height + at : d * height + at + SUB, :] for d in range(channels // SUB)]
        return jnp.concatenate(tiles, axis=0).T

    for a in range(radix):
        rows = slice(a * LANES, (a + 1) * LANES)
        conv, back, lagged = (piece(a, s) for s in range(3))
        first = gate_in[rows, :].astype(jnp.float32)
        value = value_in[rows, :].astype(jnp.float32)
        second = gate_out[rows, :].astype(jnp.float32)
        grad = cotangent[rows, :].astype(jnp.float32)
        g_out[rows, :] = (grad * (conv + gain * (first * value))).astype(g_out.dtype)
        mid = back + gain * (grad * second)
        g_in[rows, :] = (mid * value).astype(g_in.dtype)
        g_value[rows, :] = (mid * first).astype(g_value.dtype)
        g_taps[rows, :] = lagged * scale
    for d in range(channels // SUB):
        share = data[(d + 1) * height - 1 : (d + 1) * height, :SUB]
        g_skip[:, d * SUB : (d + 1) * SUB] = share * scale


PARAMS = pltpu.CompilerParams(vmem_limit_bytes=24 * 1024 * 1024)
ON_CHIP = pl.BlockSpec(memory_space=pltpu.VMEM)
IN_HBM = pl.BlockSpec(memory_space=pltpu.HBM)


def held(x):
    return x if INTERPRET else pltpu.with_memory_space_constraint(x, pltpu.HBM)


def call(kernel, out_shape, scratch=(), in_specs=None):
    extra = {} if in_specs is None else {"in_specs": in_specs}
    out_specs = jax.tree.map(lambda _: ON_CHIP, out_shape)
    return pl.pallas_call(
        kernel,
        out_shape=out_shape,
        out_specs=out_specs,
        scratch_shapes=scratch,
        compiler_params=PARAMS,
        interpret=INTERPRET,
        **extra,
    )


def pack(gate_in, value_in, gate_out, cotangent, taps):
    rows, channels = taps.shape
    height = 3 * rows // LANES * SUB
    shape = jax.ShapeDtypeStruct((channels // SUB, height, LANES), jnp.float32)
    operands = tuple(held(x) for x in (taps, gate_in, value_in, cotangent, gate_out))
    scratch = [pltpu.VMEM(x.shape, x.dtype) for x in operands]
    scratch.append(pltpu.SemaphoreType.DMA((len(operands),)))
    return call(pack_kernel, shape, scratch, [IN_HBM] * len(operands))(*operands)


def spectral(data):
    blocks = data.shape[0]
    radix = data.shape[1] // (3 * SUB)
    consts = [jnp.asarray(t) for t in tables(blocks, radix)]
    shape = jax.ShapeDtypeStruct((blocks * (3 * radix * SUB + 1), LANES), jnp.float32)
    rows = blocks * radix * SUB
    scratch = [
        pltpu.VMEM((3, radix, NEAR, FAR, 2, SUB, LANES), jnp.float32),
        pltpu.VMEM((6, rows, 6 * LANES), jnp.bfloat16),
        pltpu.VMEM((6, rows, 2 * LANES), jnp.float32),
    ]
    return call(spectral_kernel, shape, scratch)(data, *consts)


def unpack(data, gate_in, value_in, gate_out, cotangent, skip_gain, scale):
    rows, channels = gate_in.shape
    half = jax.ShapeDtypeStruct((rows, channels), jnp.bfloat16)
    shapes = (
        half,
        half,
        half,
        jax.ShapeDtypeStruct((rows, channels), jnp.float32),
        jax.ShapeDtypeStruct((1, channels), jnp.float32),
    )

    def kernel(*refs):
        unpack_kernel(*refs, scale=scale)

    outs = call(kernel, shapes)(data, gate_in, value_in, gate_out, cotangent, skip_gain[None])
    return (*outs[:4], outs[4][0])


def body(gate_in, value_in, gate_out, filter_taps, skip_gain, cotangent):
    scale = 1.0 / math.sqrt(lax.axis_size(AXES) * gate_in.shape[0])
    data = pack(gate_in, value_in, gate_out, cotangent, filter_taps)
    data = lax.all_to_all(data, AXES, split_axis=0, concat_axis=0, tiled=True)
    data = spectral(data)
    rows = data.reshape(lax.axis_size(AXES), -1, 1, LANES)
    data = lax.all_to_all(rows, AXES, split_axis=0, concat_axis=0, tiled=True).reshape(data.shape)
    return unpack(data, gate_in, value_in, gate_out, cotangent, skip_gain, scale)


def solution(mesh):
    spread = P(AXES, "ch")
    return jax.shard_map(
        body,
        mesh=mesh,
        in_specs=(spread, spread, spread, spread, P("ch"), spread),
        out_specs=(spread, spread, spread, spread, P("ch")),
        check_vma=False,
    )
```

time: 61.5 us -> 59 us (0.959)
  blocking collectives: 51.8 us -> 50.5 us
  Pallas kernels: 8.69 us -> 7.51 us
    all_to_all x2 -> x1, blocking collectives: 51.8 us -> 28.6 us  [body(): data = lax.all_to_all(data, AXES, split_axis=0, concat_axis=0, tiled=True)]
    all_to_all x0 -> x1, blocking collectives: none -> 22 us  [body(): lax.all_to_all(rows, AXES, split_axis=0, concat_axis=0, tiled=True)]
    pallas_call x1, Pallas kernels: 5.8 us -> 4.65 us  [spectral(): return call(spectral_kernel, shape, scratch)(data, *consts)]
where the time goes in v3:
time: 59 us; the launch traced here: 58.8 us
  blocking collectives  50.5 us (86%)
  Pallas kernels  7.51 us (13%)
  between operations  0.74 us (1%)
    all_to_all x1, blocking collectives, body(): data = lax.all_to_all(data, AXES, split_axis=0, concat_axis=0, tiled=True)  28.6 us
    all_to_all x1, blocking collectives, body(): lax.all_to_all(rows, AXES, split_axis=0, concat_axis=0, tiled=True)  22 us
    pallas_call x1, Pallas kernels, spectral(): return call(spectral_kernel, shape, scratch)(data, *consts)  4.65 us
    pallas_call x1, Pallas kernels, pack(): call(pack_kernel, shape, scratch, [IN_HBM] * len(operands))(*operands)  1.56 us
    pallas_call x1, Pallas kernels, unpack(): call(kernel, shapes)  1.31 us

profile of v3, /device:TPU:0, one launch (start us, length us, event | category | flops | bytes accessed | tf_op | source)
XLA Modules:
  0.0 58.8 jit_solution(8426353042070032655)
XLA Ops:
  0.6 1.6 %shard_map.128 = f32[32,72,128]{2,1,0:T(8,128)S(1)} custom-call(f32[384,256]{1,0:T(8,128)} %taps_in.1, bf16[384,256]{1,0:T(8,128)(2,1)} %refs_1_.1, bf16[384,256]{1,0:T(8,128)(2,1)} %refs_2_.1, bf16[384,256]{1,0:T(8,128)(2,1)} %refs_4_.1, bf16[384,256]{1,0:T(8,128)(2,1)} %refs_3_.1), custom_call_target="tpu_custom_call" | custom-call | tf_op jit(solution)/shard_map/pallas_call | solution.py:309
  2.2 0.0 copy-start.4
  2.2 0.0 copy-start.5
  2.2 0.0 copy-start.6
  2.2 28.6 %all_to_all.10.data = f32[32,72,128]{2,1,0:T(8,128)S(1)} all-to-all(f32[32,72,128]{2,1,0:T(8,128)S(1)} %shard_map.128), channel_id=1, replica_groups=mesh['grp'=4,'blk'=8,'ch'=4] {'grp','blk'}, dimensions={0} | all-to-all | bytes 2359296 | tf_op jit(solution)/shard_map/all_to_all | solution.py:347
  30.8 0.0 copy-done.4
  30.8 0.0 copy-done.5
  30.8 0.0 copy-done.6
  30.8 4.6 %shard_map.129 = f32[2336,128]{1,0:T(8,128)S(1)} custom-call(f32[32,72,128]{2,1,0:T(8,128)S(1)} %all_to_all.10.data, bf16[768,256]{1,0:T(8,128)(2,1)S(1)} %copy-done.6, bf16[768,256]{1,0:T(8,128)(2,1)S(1)} %copy-done.5, f32[2,96,8,128]{3,2,1,0:T(8,128)S(1)} %copy-done.4), custom_call_target="tpu_custom_call" | custom-call | tf_op jit(solution)/shard_map/pallas_call | solution.py:323
  35.5 0.0 copy-start
  35.5 0.0 copy-start.1
  35.5 0.0 copy-start.2
  35.5 0.0 copy-start.3
  35.5 0.0 copy-start.7
  35.5 22.0 %all_to_all.11 = f32[32,73,1,128]{3,2,1,0:T(1,128)S(1)} all-to-all(f32[32,73,1,128]{3,2,1,0:T(1,128)S(1)} %bitcast.5), channel_id=1, replica_groups=mesh['grp'=4,'blk'=8,'ch'=4] {'grp','blk'}, dimensions={0} | all-to-all | bytes 2392064 | tf_op jit(solution)/shard_map/all_to_all | solution.py:350
  57.5 0.0 copy-done
  57.5 0.0 copy-done.1
  57.5 0.0 copy-done.2
  57.5 0.0 copy-done.3
  57.5 0.0 copy-done.7
  57.5 1.3 %shard_map.130 = (bf16[384,256]{1,0:T(8,128)(2,1)}, bf16[384,256]{1,0:T(8,128)(2,1)}, bf16[384,256]{1,0:T(8,128)(2,1)}, f32[384,256]{1,0:T(8,128)}, f32[1,256]{1,0:T(1,128)}) custom-call(f32[2336,128]{1,0:T(8,128)S(1)} %bitcast.4, bf16[384,256]{1,0:T(8,128)(2,1)S(1)} %copy-done, bf16[384,256]{1,0:T(8,128)(2,1)S(1)} %copy-done.1, ...), custom_call_target="tpu_custom_call" | custom-call | tf_op jit(solution)/shard_map/pallas_call | solution.py:340
Async XLA Ops:
  2.2 28.6 %copy-start.4 = (f32[2,96,8,128]{3,2,1,0:T(8,128)S(1)}, f32[2,96,8,128]{3,2,1,0:T(8,128)}, u32[]{:S(2)}) copy-start(f32[2,96,8,128]{3,2,1,0:T(8,128)} %constant.8.clone.twist) | copy-start | bytes 2359300
  2.2 28.6 %copy-start.5 = (bf16[768,256]{1,0:T(8,128)(2,1)S(1)}, bf16[768,256]{1,0:T(8,128)(2,1)}, u32[]{:S(2)}) copy-start(bf16[768,256]{1,0:T(8,128)(2,1)} %constant.7.clone.lane_behind) | copy-start | bytes 1179652
  2.2 28.6 %copy-start.6 = (bf16[768,256]{1,0:T(8,128)(2,1)S(1)}, bf16[768,256]{1,0:T(8,128)(2,1)}, u32[]{:S(2)}) copy-start(bf16[768,256]{1,0:T(8,128)(2,1)} %constant.6.clone.lane_ahead) | copy-start | bytes 1179652
  35.5 22.0 %copy-start = (bf16[384,256]{1,0:T(8,128)(2,1)S(1)}, bf16[384,256]{1,0:T(8,128)(2,1)}, u32[]{:S(2)}) copy-start(bf16[384,256]{1,0:T(8,128)(2,1)} %refs_1_.1) | copy-start | bytes 589828
  35.5 22.0 %copy-start.1 = (bf16[384,256]{1,0:T(8,128)(2,1)S(1)}, bf16[384,256]{1,0:T(8,128)(2,1)}, u32[]{:S(2)}) copy-start(bf16[384,256]{1,0:T(8,128)(2,1)} %refs_2_.1) | copy-start | bytes 589828
  35.5 22.0 %copy-start.2 = (bf16[384,256]{1,0:T(8,128)(2,1)S(1)}, bf16[384,256]{1,0:T(8,128)(2,1)}, u32[]{:S(2)}) copy-start(bf16[384,256]{1,0:T(8,128)(2,1)} %refs_4_.1) | copy-start | bytes 589828
  35.5 22.0 %copy-start.3 = (bf16[384,256]{1,0:T(8,128)(2,1)S(1)}, bf16[384,256]{1,0:T(8,128)(2,1)}, u32[]{:S(2)}) copy-start(bf16[384,256]{1,0:T(8,128)(2,1)} %refs_3_.1) | copy-start | bytes 589828
  35.5 22.0 %copy-start.7 = (f32[256]{0:T(256)S(1)}, f32[256]{0:T(256)}, u32[]{:S(2)}) copy-start(f32[256]{0:T(256)} %param.13) | copy-start | bytes 3076

commit v4 on v3

--- a/solution.py
+++ b/solution.py
@@ -155,7 +155,7 @@
     def store(s, row, pairs):
         for p in range(2):
             high, low = halves(jnp.concatenate([pair[p] for pair in pairs], axis=0))
-            for j, w in enumerate((high, low, high)):
+            for j, w in enumerate((high, low)):
                 lanes = (2 * j + p) * LANES
                 gs[s, row : row + 2 * SUB, lanes : lanes + LANES] = w
 
@@ -173,6 +173,7 @@
                     re, im = turn(pair, -n0 * k1 / blocks)
                     ts[s, a, n0, k1, 0] = re
                     ts[s, a, n0, k1, 1] = im
+                yield
         for k1 in range(FAR):
             quads = [
                 four([(ts[s, a, n0, k1, 0], ts[s, a, n0, k1, 1]) for n0 in range(NEAR)], -1)
@@ -190,7 +191,7 @@
                 for e in range(radix):
                     row = (e * blocks + k1 * NEAR + k2) * SUB
                     store(s, row, [pairs[0][e], pairs[1][e]])
-        spec[s] = dot(gs[s], lane_ahead[...])
+            yield
 
     def product(s):
         left, right = ((1, 0), (1, 2), (0, 2))[s]
@@ -203,10 +204,11 @@
                 both = lr * rr + li * ri, lr * ri - li * rr
             for p in range(2):
                 high, low = halves(both[p])
-                for j, w in enumerate((high, low, high)):
+                for j, w in enumerate((high, low)):
                     lanes = (2 * j + p) * LANES
                     gs[3 + s, row : row + 2 * SUB, lanes : lanes + LANES] = w
-        spec[3 + s] = dot(gs[3 + s], lane_behind[...])
+            if row % (6 * SUB) == 0:
+                yield
 
     def backward(s):
         for k1 in range(FAR):
@@ -225,6 +227,7 @@
                     re, im = turn(pair, n0 * k1 / blocks)
                     ts[s, a, n0, k1, 0] = re
                     ts[s, a, n0, k1, 1] = im
+            yield
         for a in range(radix):
             for n0 in range(NEAR):
                 values = eight([(ts[s, a, n0, k1, 0], ts[s, a, n0, k1, 1]) for k1 in range(FAR)], 1)
@@ -234,16 +237,34 @@
                     angle = 2.0 * math.pi * (radix * d + a) / (4 * span)
                     row = d * height + (a * 3 + s) * SUB
                     out[row : row + SUB, :] = (scale * math.cos(angle)) * re - (scale * math.sin(angle)) * im
-
-    forward(0)
-    forward(1)
-    product(0)
-    forward(2)
-    backward(0)
-    product(1)
-    product(2)
-    backward(1)
-    backward(2)
+                yield
+
+    def lane_dots(s, table):
+        step = rows // 3
+        for row in range(0, rows, step):
+            left = gs[s, row : row + step]
+            main = dot(left, table[: 4 * LANES])
+            spec[s, row : row + step] = main + dot(left[:, : 2 * LANES], table[4 * LANES :])
+            yield
+
+    def mix(vector, *dots):
+        gap = max(1, 18 // max(1, 3 * len(dots)))
+        chain = (piece for step in dots for piece in step)
+        for count, _ in enumerate(vector):
+            if count % gap == 0:
+                next(chain, None)
+        for _ in chain:
+            pass
+
+    mix(forward(0))
+    mix(forward(1), lane_dots(0, lane_ahead))
+    mix(forward(2), lane_dots(1, lane_ahead))
+    mix(product(0), lane_dots(2, lane_ahead))
+    mix(product(1), lane_dots(3, lane_behind))
+    mix(product(2), lane_dots(4, lane_behind))
+    mix(backward(0), lane_dots(5, lane_behind))
+    mix(backward(1))
+    mix(backward(2))
 
 
 def unpack_kernel(
@@ -317,7 +338,7 @@
     rows = blocks * radix * SUB
     scratch = [
         pltpu.VMEM((3, radix, NEAR, FAR, 2, SUB, LANES), jnp.float32),
-        pltpu.VMEM((6, rows, 6 * LANES), jnp.bfloat16),
+        pltpu.VMEM((6, rows, 4 * LANES), jnp.bfloat16),
         pltpu.VMEM((6, rows, 2 * LANES), jnp.float32),
     ]
     return call(spectral_kernel, shape, scratch)(data, *consts)

time: 59 us -> 58.6 us (level)
  no operation moved by 1% of the time
where the time goes in v4:
time: 58.6 us; the launch traced here: 58.4 us
  blocking collectives  50.5 us (86%)
  Pallas kernels  7.1 us (12%)
  between operations  0.74 us (1%)
    all_to_all x1, blocking collectives, body(): data = lax.all_to_all(data, AXES, split_axis=0, concat_axis=0, tiled=True)  28.6 us
    all_to_all x1, blocking collectives, body(): lax.all_to_all(rows, AXES, split_axis=0, concat_axis=0, tiled=True)  22 us
    pallas_call x1, Pallas kernels, spectral(): return call(spectral_kernel, shape, scratch)(data, *consts)  4.24 us
    pallas_call x1, Pallas kernels, pack(): call(pack_kernel, shape, scratch, [IN_HBM] * len(operands))(*operands)  1.56 us
    pallas_call x1, Pallas kernels, unpack(): call(kernel, shapes)  1.31 us

profile of v4, /device:TPU:0, one launch (start us, length us, event | category | flops | bytes accessed | tf_op | source)
XLA Modules:
  0.0 58.4 jit_solution(1376605850790411661)
XLA Ops:
  0.6 1.6 %shard_map.128 = f32[32,72,128]{2,1,0:T(8,128)S(1)} custom-call(f32[384,256]{1,0:T(8,128)} %taps_in.1, bf16[384,256]{1,0:T(8,128)(2,1)} %refs_1_.1, bf16[384,256]{1,0:T(8,128)(2,1)} %refs_2_.1, bf16[384,256]{1,0:T(8,128)(2,1)} %refs_4_.1, bf16[384,256]{1,0:T(8,128)(2,1)} %refs_3_.1), custom_call_target="tpu_custom_call" | custom-call | tf_op jit(solution)/shard_map/pallas_call | solution.py:330
  2.2 0.0 copy-start.4
  2.2 0.0 copy-start.5
  2.2 0.0 copy-start.6
  2.2 28.6 %all_to_all.10.data = f32[32,72,128]{2,1,0:T(8,128)S(1)} all-to-all(f32[32,72,128]{2,1,0:T(8,128)S(1)} %shard_map.128), channel_id=1, replica_groups=mesh['grp'=4,'blk'=8,'ch'=4] {'grp','blk'}, dimensions={0} | all-to-all | bytes 2359296 | tf_op jit(solution)/shard_map/all_to_all | solution.py:368
  30.8 0.0 copy-done.4
  30.8 0.0 copy-done.5
  30.8 0.0 copy-done.6
  30.8 4.2 %shard_map.129 = f32[2336,128]{1,0:T(8,128)S(1)} custom-call(f32[32,72,128]{2,1,0:T(8,128)S(1)} %all_to_all.10.data, bf16[768,256]{1,0:T(8,128)(2,1)S(1)} %copy-done.6, bf16[768,256]{1,0:T(8,128)(2,1)S(1)} %copy-done.5, f32[2,96,8,128]{3,2,1,0:T(8,128)S(1)} %copy-done.4), custom_call_target="tpu_custom_call" | custom-call | tf_op jit(solution)/shard_map/pallas_call | solution.py:344
  35.0 0.0 copy-start
  35.1 0.0 copy-start.1
  35.1 0.0 copy-start.2
  35.1 0.0 copy-start.3
  35.1 0.0 copy-start.7
  35.1 22.0 %all_to_all.11 = f32[32,73,1,128]{3,2,1,0:T(1,128)S(1)} all-to-all(f32[32,73,1,128]{3,2,1,0:T(1,128)S(1)} %bitcast.5), channel_id=1, replica_groups=mesh['grp'=4,'blk'=8,'ch'=4] {'grp','blk'}, dimensions={0} | all-to-all | bytes 2392064 | tf_op jit(solution)/shard_map/all_to_all | solution.py:371
  57.1 0.0 copy-done
  57.1 0.0 copy-done.1
  57.1 0.0 copy-done.2
  57.1 0.0 copy-done.3
  57.1 0.0 copy-done.7
  57.1 1.3 %shard_map.130 = (bf16[384,256]{1,0:T(8,128)(2,1)}, bf16[384,256]{1,0:T(8,128)(2,1)}, bf16[384,256]{1,0:T(8,128)(2,1)}, f32[384,256]{1,0:T(8,128)}, f32[1,256]{1,0:T(1,128)}) custom-call(f32[2336,128]{1,0:T(8,128)S(1)} %bitcast.4, bf16[384,256]{1,0:T(8,128)(2,1)S(1)} %copy-done, bf16[384,256]{1,0:T(8,128)(2,1)S(1)} %copy-done.1, ...), custom_call_target="tpu_custom_call" | custom-call | tf_op jit(solution)/shard_map/pallas_call | solution.py:361
Async XLA Ops:
  2.2 28.6 %copy-start.4 = (f32[2,96,8,128]{3,2,1,0:T(8,128)S(1)}, f32[2,96,8,128]{3,2,1,0:T(8,128)}, u32[]{:S(2)}) copy-start(f32[2,96,8,128]{3,2,1,0:T(8,128)} %constant.8.clone.twist) | copy-start | bytes 2359300
  2.2 28.6 %copy-start.5 = (bf16[768,256]{1,0:T(8,128)(2,1)S(1)}, bf16[768,256]{1,0:T(8,128)(2,1)}, u32[]{:S(2)}) copy-start(bf16[768,256]{1,0:T(8,128)(2,1)} %constant.7.clone.lane_behind) | copy-start | bytes 1179652
  2.2 28.6 %copy-start.6 = (bf16[768,256]{1,0:T(8,128)(2,1)S(1)}, bf16[768,256]{1,0:T(8,128)(2,1)}, u32[]{:S(2)}) copy-start(bf16[768,256]{1,0:T(8,128)(2,1)} %constant.6.clone.lane_ahead) | copy-start | bytes 1179652
  35.0 22.0 %copy-start = (bf16[384,256]{1,0:T(8,128)(2,1)S(1)}, bf16[384,256]{1,0:T(8,128)(2,1)}, u32[]{:S(2)}) copy-start(bf16[384,256]{1,0:T(8,128)(2,1)} %refs_1_.1) | copy-start | bytes 589828
  35.1 22.0 %copy-start.1 = (bf16[384,256]{1,0:T(8,128)(2,1)S(1)}, bf16[384,256]{1,0:T(8,128)(2,1)}, u32[]{:S(2)}) copy-start(bf16[384,256]{1,0:T(8,128)(2,1)} %refs_2_.1) | copy-start | bytes 589828
  35.1 22.0 %copy-start.2 = (bf16[384,256]{1,0:T(8,128)(2,1)S(1)}, bf16[384,256]{1,0:T(8,128)(2,1)}, u32[]{:S(2)}) copy-start(bf16[384,256]{1,0:T(8,128)(2,1)} %refs_4_.1) | copy-start | bytes 589828
  35.1 22.0 %copy-start.3 = (bf16[384,256]{1,0:T(8,128)(2,1)S(1)}, bf16[384,256]{1,0:T(8,128)(2,1)}, u32[]{:S(2)}) copy-start(bf16[384,256]{1,0:T(8,128)(2,1)} %refs_3_.1) | copy-start | bytes 589828
  35.1 22.0 %copy-start.7 = (f32[256]{0:T(256)S(1)}, f32[256]{0:T(256)}, u32[]{:S(2)}) copy-start(f32[256]{0:T(256)} %param.13) | copy-start | bytes 3076

commit v5 on v4

--- a/solution.py
+++ b/solution.py
@@ -8,7 +8,8 @@
 from jax.experimental.pallas import tpu as pltpu
 from jax.sharding import PartitionSpec as P
 
-AXES = ("grp", "blk")
+PLACE = ("grp", "far", "near")
+AXES = ("grp", "near", "far")
 LANES = 128
 SUB = 8
 INTERPRET = False
@@ -134,7 +135,7 @@
     send(2, lambda r: grad[r, :].astype(jnp.float32) * second[r, :].astype(jnp.float32))
 
 
-def spectral_kernel(data, lane_ahead, lane_behind, twist, out, ts, gs, spec):
+def spectral_kernel(data, lane_ahead, lane_behind, twist, out, ts, gs, spec, *, slots):
     blocks = data.shape[0]
     radix = data.shape[1] // (3 * SUB)
     span = blocks * radix
@@ -166,7 +167,7 @@
                 for n1 in range(FAR):
                     m = NEAR * n1 + n0
                     d = ((m - a) * pow(radix, -1, blocks)) % blocks
-                    x = data[d, at(a, s), :]
+                    x = data[slots[d], at(a, s), :]
                     angle = 2.0 * math.pi * (radix * d + a) / (4 * span)
                     values.append((math.cos(angle) * x, -math.sin(angle) * x))
                 for k1, pair in enumerate(eight(values, -1)):
@@ -235,7 +236,7 @@
                     m = NEAR * n1 + n0
                     d = ((m - a) * pow(radix, -1, blocks)) % blocks
                     angle = 2.0 * math.pi * (radix * d + a) / (4 * span)
-                    row = d * height + (a * 3 + s) * SUB
+                    row = slots[d] * height + (a * 3 + s) * SUB
                     out[row : row + SUB, :] = (scale * math.cos(angle)) * re - (scale * math.sin(angle)) * im
                 yield
 
@@ -330,7 +331,7 @@
     return call(pack_kernel, shape, scratch, [IN_HBM] * len(operands))(*operands)
 
 
-def spectral(data):
+def spectral(data, slots):
     blocks = data.shape[0]
     radix = data.shape[1] // (3 * SUB)
     consts = [jnp.asarray(t) for t in tables(blocks, radix)]
@@ -341,7 +342,11 @@
         pltpu.VMEM((6, rows, 4 * LANES), jnp.bfloat16),
         pltpu.VMEM((6, rows, 2 * LANES), jnp.float32),
     ]
-    return call(spectral_kernel, shape, scratch)(data, *consts)
+
+    def kernel(*refs):
+        spectral_kernel(*refs, slots=slots)
+
+    return call(kernel, shape, scratch)(data, *consts)
 
 
 def unpack(data, gate_in, value_in, gate_out, cotangent, skip_gain, scale):
@@ -366,17 +371,24 @@
     scale = 1.0 / math.sqrt(lax.axis_size(AXES) * gate_in.shape[0])
     data = pack(gate_in, value_in, gate_out, cotangent, filter_taps)
     data = lax.all_to_all(data, AXES, split_axis=0, concat_axis=0, tiled=True)
-    data = spectral(data)
+    sizes = [lax.axis_size(name) for name in PLACE]
+    order = [PLACE.index(name) for name in AXES]
+    slots = np.arange(math.prod(sizes)).reshape([sizes[i] for i in order])
+    slots = [int(i) for i in slots.transpose(np.argsort(order)).reshape(-1)]
+    data = spectral(data, slots)
     rows = data.reshape(lax.axis_size(AXES), -1, 1, LANES)
     data = lax.all_to_all(rows, AXES, split_axis=0, concat_axis=0, tiled=True).reshape(data.shape)
     return unpack(data, gate_in, value_in, gate_out, cotangent, skip_gain, scale)
 
 
 def solution(mesh):
-    spread = P(AXES, "ch")
+    near = 2
+    grp, blk, ch = (mesh.shape[name] for name in ("grp", "blk", "ch"))
+    split = jax.sharding.Mesh(mesh.devices.reshape(grp, blk // near, near, ch), (*PLACE, "ch"))
+    spread = P(PLACE, "ch")
     return jax.shard_map(
         body,
-        mesh=mesh,
+        mesh=split,
         in_specs=(spread, spread, spread, spread, P("ch"), spread),
         out_specs=(spread, spread, spread, spread, P("ch")),
         check_vma=False,

time: 58.6 us -> 58.5 us (level)
  no operation moved by 1% of the time
where the time goes in v5:
time: 58.5 us; the launch traced here: 58.3 us
  blocking collectives  50.4 us (86%)
  Pallas kernels  7.1 us (12%)
  between operations  0.74 us (1%)
    all_to_all x1, blocking collectives, body(): data = lax.all_to_all(data, AXES, split_axis=0, concat_axis=0, tiled=True)  28.5 us
    all_to_all x1, blocking collectives, body(): lax.all_to_all(rows, AXES, split_axis=0, concat_axis=0, tiled=True)  21.9 us
    pallas_call x1, Pallas kernels, spectral(): return call(kernel, shape, scratch)(data, *consts)  4.23 us
    pallas_call x1, Pallas kernels, pack(): call(pack_kernel, shape, scratch, [IN_HBM] * len(operands))(*operands)  1.56 us
    pallas_call x1, Pallas kernels, unpack(): call(kernel, shapes)  1.31 us

profile of v5, /device:TPU:0, one launch (start us, length us, event | category | flops | bytes accessed | tf_op | source)
XLA Modules:
  0.0 58.3 jit_solution(15165474573423772307)
XLA Ops:
  0.6 1.6 %shard_map.128 = f32[32,72,128]{2,1,0:T(8,128)S(1)} custom-call(f32[384,256]{1,0:T(8,128)} %taps_in.1, bf16[384,256]{1,0:T(8,128)(2,1)} %refs_1_.2, bf16[384,256]{1,0:T(8,128)(2,1)} %refs_2_.2, bf16[384,256]{1,0:T(8,128)(2,1)} %refs_4_.1, bf16[384,256]{1,0:T(8,128)(2,1)} %refs_3_.2), custom_call_target="tpu_custom_call" | custom-call | tf_op jit(solution)/shard_map/pallas_call | solution.py:331
  2.2 0.0 copy-start.4
  2.2 0.0 copy-start.5
  2.2 0.0 copy-start.6
  2.2 28.5 %all_to_all.10.refs_0_ = f32[32,72,128]{2,1,0:T(8,128)S(1)} all-to-all(f32[32,72,128]{2,1,0:T(8,128)S(1)} %shard_map.128), channel_id=1, replica_groups=mesh['grp'=4,'far'=4,'near'=2,'ch'=4] {'grp','near','far'}, dimensions={0} | all-to-all | bytes 2359296 | tf_op jit(solution)/shard_map/all_to_all | solution.py:373
  30.7 0.0 copy-done.4
  30.7 0.0 copy-done.5
  30.7 0.0 copy-done.6
  30.7 4.2 %shard_map.129 = f32[2336,128]{1,0:T(8,128)S(1)} custom-call(f32[32,72,128]{2,1,0:T(8,128)S(1)} %all_to_all.10.refs_0_, bf16[768,256]{1,0:T(8,128)(2,1)S(1)} %copy-done.6, bf16[768,256]{1,0:T(8,128)(2,1)S(1)} %copy-done.5, f32[2,96,8,128]{3,2,1,0:T(8,128)S(1)} %copy-done.4), custom_call_target="tpu_custom_call" | custom-call | tf_op jit(solution)/shard_map/pallas_call | solution.py:349
  35.0 0.0 copy-start
  35.0 0.0 copy-start.1
  35.0 0.0 copy-start.2
  35.0 0.0 copy-start.3
  35.0 0.0 copy-start.7
  35.0 21.9 %all_to_all.11 = f32[32,73,1,128]{3,2,1,0:T(1,128)S(1)} all-to-all(f32[32,73,1,128]{3,2,1,0:T(1,128)S(1)} %bitcast.5), channel_id=1, replica_groups=mesh['grp'=4,'far'=4,'near'=2,'ch'=4] {'grp','near','far'}, dimensions={0} | all-to-all | bytes 2392064 | tf_op jit(solution)/shard_map/all_to_all | solution.py:380
  56.9 0.0 copy-done
  56.9 0.0 copy-done.1
  56.9 0.0 copy-done.2
  56.9 0.0 copy-done.3
  56.9 0.0 copy-done.7
  57.0 1.3 %shard_map.130 = (bf16[384,256]{1,0:T(8,128)(2,1)}, bf16[384,256]{1,0:T(8,128)(2,1)}, bf16[384,256]{1,0:T(8,128)(2,1)}, f32[384,256]{1,0:T(8,128)}, f32[1,256]{1,0:T(1,128)}) custom-call(f32[2336,128]{1,0:T(8,128)S(1)} %bitcast.4, bf16[384,256]{1,0:T(8,128)(2,1)S(1)} %copy-done, bf16[384,256]{1,0:T(8,128)(2,1)S(1)} %copy-done.1, ...), custom_call_target="tpu_custom_call" | custom-call | tf_op jit(solution)/shard_map/pallas_call | solution.py:366
Async XLA Ops:
  2.2 28.5 %copy-start.4 = (f32[2,96,8,128]{3,2,1,0:T(8,128)S(1)}, f32[2,96,8,128]{3,2,1,0:T(8,128)}, u32[]{:S(2)}) copy-start(f32[2,96,8,128]{3,2,1,0:T(8,128)} %constant.8.clone.refs_3_) | copy-start | bytes 2359300
  2.2 28.5 %copy-start.5 = (bf16[768,256]{1,0:T(8,128)(2,1)S(1)}, bf16[768,256]{1,0:T(8,128)(2,1)}, u32[]{:S(2)}) copy-start(bf16[768,256]{1,0:T(8,128)(2,1)} %constant.7.clone.refs_2_) | copy-start | bytes 1179652
  2.2 28.5 %copy-start.6 = (bf16[768,256]{1,0:T(8,128)(2,1)S(1)}, bf16[768,256]{1,0:T(8,128)(2,1)}, u32[]{:S(2)}) copy-start(bf16[768,256]{1,0:T(8,128)(2,1)} %constant.6.clone.refs_1_) | copy-start | bytes 1179652
  35.0 21.9 %copy-start = (bf16[384,256]{1,0:T(8,128)(2,1)S(1)}, bf16[384,256]{1,0:T(8,128)(2,1)}, u32[]{:S(2)}) copy-start(bf16[384,256]{1,0:T(8,128)(2,1)} %refs_1_.2) | copy-start | bytes 589828
  35.0 21.9 %copy-start.1 = (bf16[384,256]{1,0:T(8,128)(2,1)S(1)}, bf16[384,256]{1,0:T(8,128)(2,1)}, u32[]{:S(2)}) copy-start(bf16[384,256]{1,0:T(8,128)(2,1)} %refs_2_.2) | copy-start | bytes 589828
  35.0 21.9 %copy-start.2 = (bf16[384,256]{1,0:T(8,128)(2,1)S(1)}, bf16[384,256]{1,0:T(8,128)(2,1)}, u32[]{:S(2)}) copy-start(bf16[384,256]{1,0:T(8,128)(2,1)} %refs_4_.1) | copy-start | bytes 589828
  35.0 21.9 %copy-start.3 = (bf16[384,256]{1,0:T(8,128)(2,1)S(1)}, bf16[384,256]{1,0:T(8,128)(2,1)}, u32[]{:S(2)}) copy-start(bf16[384,256]{1,0:T(8,128)(2,1)} %refs_3_.2) | copy-start | bytes 589828
  35.0 21.9 %copy-start.7 = (f32[256]{0:T(256)S(1)}, f32[256]{0:T(256)}, u32[]{:S(2)}) copy-start(f32[256]{0:T(256)} %param.13) | copy-start | bytes 3076

commit v6 on v4

--- a/solution.py
+++ b/solution.py
@@ -292,9 +292,14 @@
         g_in[rows, :] = (mid * value).astype(g_in.dtype)
         g_value[rows, :] = (mid * first).astype(g_value.dtype)
         g_taps[rows, :] = lagged * scale
-    for d in range(channels // SUB):
-        share = data[(d + 1) * height - 1 : (d + 1) * height, :SUB]
-        g_skip[:, d * SUB : (d + 1) * SUB] = share * scale
+    owner = lax.broadcasted_iota(jnp.int32, (1, LANES), 1) // SUB
+    group = LANES // SUB
+    for h in range(channels // LANES):
+        picked = jnp.zeros((1, LANES), jnp.float32)
+        for j in range(group):
+            end = (h * group + j + 1) * height
+            picked = jnp.where(owner == j, data[end - 1 : end, :], picked)
+        g_skip[:, h * LANES : (h + 1) * LANES] = picked * scale
 
 
 PARAMS = pltpu.CompilerParams(vmem_limit_bytes=24 * 1024 * 1024)

time: 58.6 us -> 58.6 us (level)
  no operation moved by 1% of the time
where the time goes in v6:
time: 58.6 us; the launch traced here: 58.4 us
  blocking collectives  50.5 us (86%)
  Pallas kernels  7.09 us (12%)
  between operations  0.74 us (1%)
    all_to_all x1, blocking collectives, body(): data = lax.all_to_all(data, AXES, split_axis=0, concat_axis=0, tiled=True)  28.6 us
    all_to_all x1, blocking collectives, body(): lax.all_to_all(rows, AXES, split_axis=0, concat_axis=0, tiled=True)  22 us
    pallas_call x1, Pallas kernels, spectral(): return call(spectral_kernel, shape, scratch)(data, *consts)  4.24 us
    pallas_call x1, Pallas kernels, pack(): call(pack_kernel, shape, scratch, [IN_HBM] * len(operands))(*operands)  1.56 us
    pallas_call x1, Pallas kernels, unpack(): call(kernel, shapes)  1.3 us

profile of v6, /device:TPU:0, one launch (start us, length us, event | category | flops | bytes accessed | tf_op | source)
XLA Modules:
  0.0 58.4 jit_solution(7694776029864470869)
XLA Ops:
  0.6 1.6 %shard_map.128 = f32[32,72,128]{2,1,0:T(8,128)S(1)} custom-call(f32[384,256]{1,0:T(8,128)} %taps_in.1, bf16[384,256]{1,0:T(8,128)(2,1)} %refs_1_.1, bf16[384,256]{1,0:T(8,128)(2,1)} %refs_2_.1, bf16[384,256]{1,0:T(8,128)(2,1)} %refs_4_.1, bf16[384,256]{1,0:T(8,128)(2,1)} %refs_3_.1), custom_call_target="tpu_custom_call" | custom-call | tf_op jit(solution)/shard_map/pallas_call | solution.py:335
  2.2 0.0 copy-start.4
  2.2 0.0 copy-start.5
  2.2 0.0 copy-start.6
  2.2 28.6 %all_to_all.10.data = f32[32,72,128]{2,1,0:T(8,128)S(1)} all-to-all(f32[32,72,128]{2,1,0:T(8,128)S(1)} %shard_map.128), channel_id=1, replica_groups=mesh['grp'=4,'blk'=8,'ch'=4] {'grp','blk'}, dimensions={0} | all-to-all | bytes 2359296 | tf_op jit(solution)/shard_map/all_to_all | solution.py:373
  30.8 0.0 copy-done.4
  30.8 0.0 copy-done.5
  30.8 0.0 copy-done.6
  30.8 4.2 %shard_map.129 = f32[2336,128]{1,0:T(8,128)S(1)} custom-call(f32[32,72,128]{2,1,0:T(8,128)S(1)} %all_to_all.10.data, bf16[768,256]{1,0:T(8,128)(2,1)S(1)} %copy-done.6, bf16[768,256]{1,0:T(8,128)(2,1)S(1)} %copy-done.5, f32[2,96,8,128]{3,2,1,0:T(8,128)S(1)} %copy-done.4), custom_call_target="tpu_custom_call" | custom-call | tf_op jit(solution)/shard_map/pallas_call | solution.py:349
  35.0 0.0 copy-start
  35.1 0.0 copy-start.1
  35.1 0.0 copy-start.2
  35.1 0.0 copy-start.3
  35.1 0.0 copy-start.7
  35.1 22.0 %all_to_all.11 = f32[32,73,1,128]{3,2,1,0:T(1,128)S(1)} all-to-all(f32[32,73,1,128]{3,2,1,0:T(1,128)S(1)} %bitcast.5), channel_id=1, replica_groups=mesh['grp'=4,'blk'=8,'ch'=4] {'grp','blk'}, dimensions={0} | all-to-all | bytes 2392064 | tf_op jit(solution)/shard_map/all_to_all | solution.py:376
  57.1 0.0 copy-done
  57.1 0.0 copy-done.1
  57.1 0.0 copy-done.2
  57.1 0.0 copy-done.3
  57.1 0.0 copy-done.7
  57.1 1.3 %shard_map.130 = (bf16[384,256]{1,0:T(8,128)(2,1)}, bf16[384,256]{1,0:T(8,128)(2,1)}, bf16[384,256]{1,0:T(8,128)(2,1)}, f32[384,256]{1,0:T(8,128)}, f32[1,256]{1,0:T(1,128)}) custom-call(f32[2336,128]{1,0:T(8,128)S(1)} %bitcast.4, bf16[384,256]{1,0:T(8,128)(2,1)S(1)} %copy-done, bf16[384,256]{1,0:T(8,128)(2,1)S(1)} %copy-done.1, ...), custom_call_target="tpu_custom_call" | custom-call | tf_op jit(solution)/shard_map/pallas_call | solution.py:366
Async XLA Ops:
  2.2 28.6 %copy-start.4 = (f32[2,96,8,128]{3,2,1,0:T(8,128)S(1)}, f32[2,96,8,128]{3,2,1,0:T(8,128)}, u32[]{:S(2)}) copy-start(f32[2,96,8,128]{3,2,1,0:T(8,128)} %constant.8.clone.twist) | copy-start | bytes 2359300
  2.2 28.6 %copy-start.5 = (bf16[768,256]{1,0:T(8,128)(2,1)S(1)}, bf16[768,256]{1,0:T(8,128)(2,1)}, u32[]{:S(2)}) copy-start(bf16[768,256]{1,0:T(8,128)(2,1)} %constant.7.clone.lane_behind) | copy-start | bytes 1179652
  2.2 28.6 %copy-start.6 = (bf16[768,256]{1,0:T(8,128)(2,1)S(1)}, bf16[768,256]{1,0:T(8,128)(2,1)}, u32[]{:S(2)}) copy-start(bf16[768,256]{1,0:T(8,128)(2,1)} %constant.6.clone.lane_ahead) | copy-start | bytes 1179652
  35.0 22.0 %copy-start = (bf16[384,256]{1,0:T(8,128)(2,1)S(1)}, bf16[384,256]{1,0:T(8,128)(2,1)}, u32[]{:S(2)}) copy-start(bf16[384,256]{1,0:T(8,128)(2,1)} %refs_1_.1) | copy-start | bytes 589828
  35.1 22.0 %copy-start.1 = (bf16[384,256]{1,0:T(8,128)(2,1)S(1)}, bf16[384,256]{1,0:T(8,128)(2,1)}, u32[]{:S(2)}) copy-start(bf16[384,256]{1,0:T(8,128)(2,1)} %refs_2_.1) | copy-start | bytes 589828
  35.1 22.0 %copy-start.2 = (bf16[384,256]{1,0:T(8,128)(2,1)S(1)}, bf16[384,256]{1,0:T(8,128)(2,1)}, u32[]{:S(2)}) copy-start(bf16[384,256]{1,0:T(8,128)(2,1)} %refs_4_.1) | copy-start | bytes 589828
  35.1 22.0 %copy-start.3 = (bf16[384,256]{1,0:T(8,128)(2,1)S(1)}, bf16[384,256]{1,0:T(8,128)(2,1)}, u32[]{:S(2)}) copy-start(bf16[384,256]{1,0:T(8,128)(2,1)} %refs_3_.1) | copy-start | bytes 589828
  35.1 22.0 %copy-start.7 = (f32[256]{0:T(256)S(1)}, f32[256]{0:T(256)}, u32[]{:S(2)}) copy-start(f32[256]{0:T(256)} %param.13) | copy-start | bytes 3076

commit v7 on v4

--- a/solution.py
+++ b/solution.py
@@ -113,7 +113,11 @@
     sources = (taps_in, gate_in, value_in, cotangent_in, gate_out_in)
     buffers, sems = scratch[:5], scratch[5]
     copies = [pltpu.make_async_copy(src, dst, sems.at[i]) for i, (src, dst) in enumerate(zip(sources, buffers))]
-    for copy in copies:
+    half = taps_in.shape[0] // 2
+    upper, lower = pl.ds(0, half), pl.ds(half, taps_in.shape[0] - half)
+    copies[0] = pltpu.make_async_copy(taps_in.at[upper], buffers[0].at[upper], sems.at[0])
+    tail = pltpu.make_async_copy(taps_in.at[lower], buffers[0].at[lower], sems.at[5])
+    for copy in (copies[0], tail, *copies[1:]):
         copy.start()
     radix = taps_in.shape[0] // LANES
     taps, first, value, grad, second = buffers
@@ -125,6 +129,7 @@
             out[:, at : at + SUB, :] = turned.reshape(-1, SUB, LANES)
 
     copies[0].wait()
+    tail.wait()
     send(1, lambda r: taps[r, :])
     copies[1].wait()
     copies[2].wait()
@@ -326,7 +331,7 @@
     shape = jax.ShapeDtypeStruct((channels // SUB, height, LANES), jnp.float32)
     operands = tuple(held(x) for x in (taps, gate_in, value_in, cotangent, gate_out))
     scratch = [pltpu.VMEM(x.shape, x.dtype) for x in operands]
-    scratch.append(pltpu.SemaphoreType.DMA((len(operands),)))
+    scratch.append(pltpu.SemaphoreType.DMA((len(operands) + 1,)))
     return call(pack_kernel, shape, scratch, [IN_HBM] * len(operands))(*operands)
 
 

time: 58.6 us -> 58.7 us (level)
  no operation moved by 1% of the time
where the time goes in v7:
time: 58.7 us; the launch traced here: 58.5 us
  blocking collectives  50.5 us (86%)
  Pallas kernels  7.16 us (12%)
  between operations  0.74 us (1%)
    all_to_all x1, blocking collectives, body(): data = lax.all_to_all(data, AXES, split_axis=0, concat_axis=0, tiled=True)  28.6 us
    all_to_all x1, blocking collectives, body(): lax.all_to_all(rows, AXES, split_axis=0, concat_axis=0, tiled=True)  22 us
    pallas_call x1, Pallas kernels, spectral(): return call(spectral_kernel, shape, scratch)(data, *consts)  4.23 us
    pallas_call x1, Pallas kernels, pack(): call(pack_kernel, shape, scratch, [IN_HBM] * len(operands))(*operands)  1.62 us
    pallas_call x1, Pallas kernels, unpack(): call(kernel, shapes)  1.31 us

profile of v7, /device:TPU:0, one launch (start us, length us, event | category | flops | bytes accessed | tf_op | source)
XLA Modules:
  0.0 58.5 jit_solution(16169280447326125137)
XLA Ops:
  0.6 1.6 %shard_map.128 = f32[32,72,128]{2,1,0:T(8,128)S(1)} custom-call(f32[384,256]{1,0:T(8,128)} %taps_in.1, bf16[384,256]{1,0:T(8,128)(2,1)} %refs_1_.1, bf16[384,256]{1,0:T(8,128)(2,1)} %refs_2_.1, bf16[384,256]{1,0:T(8,128)(2,1)} %refs_4_.1, bf16[384,256]{1,0:T(8,128)(2,1)} %refs_3_.1), custom_call_target="tpu_custom_call" | custom-call | tf_op jit(solution)/shard_map/pallas_call | solution.py:335
  2.3 0.0 copy-start.4
  2.3 0.0 copy-start.5
  2.3 0.0 copy-start.6
  2.3 28.6 %all_to_all.10.data = f32[32,72,128]{2,1,0:T(8,128)S(1)} all-to-all(f32[32,72,128]{2,1,0:T(8,128)S(1)} %shard_map.128), channel_id=1, replica_groups=mesh['grp'=4,'blk'=8,'ch'=4] {'grp','blk'}, dimensions={0} | all-to-all | bytes 2359296 | tf_op jit(solution)/shard_map/all_to_all | solution.py:373
  30.9 0.0 copy-done.4
  30.9 0.0 copy-done.5
  30.9 0.0 copy-done.6
  30.9 4.2 %shard_map.129 = f32[2336,128]{1,0:T(8,128)S(1)} custom-call(f32[32,72,128]{2,1,0:T(8,128)S(1)} %all_to_all.10.data, bf16[768,256]{1,0:T(8,128)(2,1)S(1)} %copy-done.6, bf16[768,256]{1,0:T(8,128)(2,1)S(1)} %copy-done.5, f32[2,96,8,128]{3,2,1,0:T(8,128)S(1)} %copy-done.4), custom_call_target="tpu_custom_call" | custom-call | tf_op jit(solution)/shard_map/pallas_call | solution.py:349
  35.1 0.0 copy-start
  35.1 0.0 copy-start.1
  35.1 0.0 copy-start.2
  35.1 0.0 copy-start.3
  35.2 0.0 copy-start.7
  35.2 22.0 %all_to_all.11 = f32[32,73,1,128]{3,2,1,0:T(1,128)S(1)} all-to-all(f32[32,73,1,128]{3,2,1,0:T(1,128)S(1)} %bitcast.5), channel_id=1, replica_groups=mesh['grp'=4,'blk'=8,'ch'=4] {'grp','blk'}, dimensions={0} | all-to-all | bytes 2392064 | tf_op jit(solution)/shard_map/all_to_all | solution.py:376
  57.1 0.0 copy-done
  57.1 0.0 copy-done.1
  57.1 0.0 copy-done.2
  57.1 0.0 copy-done.3
  57.1 0.0 copy-done.7
  57.1 1.3 %shard_map.130 = (bf16[384,256]{1,0:T(8,128)(2,1)}, bf16[384,256]{1,0:T(8,128)(2,1)}, bf16[384,256]{1,0:T(8,128)(2,1)}, f32[384,256]{1,0:T(8,128)}, f32[1,256]{1,0:T(1,128)}) custom-call(f32[2336,128]{1,0:T(8,128)S(1)} %bitcast.4, bf16[384,256]{1,0:T(8,128)(2,1)S(1)} %copy-done, bf16[384,256]{1,0:T(8,128)(2,1)S(1)} %copy-done.1, ...), custom_call_target="tpu_custom_call" | custom-call | tf_op jit(solution)/shard_map/pallas_call | solution.py:366
Async XLA Ops:
  2.3 28.6 %copy-start.4 = (f32[2,96,8,128]{3,2,1,0:T(8,128)S(1)}, f32[2,96,8,128]{3,2,1,0:T(8,128)}, u32[]{:S(2)}) copy-start(f32[2,96,8,128]{3,2,1,0:T(8,128)} %constant.8.clone.twist) | copy-start | bytes 2359300
  2.3 28.6 %copy-start.5 = (bf16[768,256]{1,0:T(8,128)(2,1)S(1)}, bf16[768,256]{1,0:T(8,128)(2,1)}, u32[]{:S(2)}) copy-start(bf16[768,256]{1,0:T(8,128)(2,1)} %constant.7.clone.lane_behind) | copy-start | bytes 1179652
  2.3 28.6 %copy-start.6 = (bf16[768,256]{1,0:T(8,128)(2,1)S(1)}, bf16[768,256]{1,0:T(8,128)(2,1)}, u32[]{:S(2)}) copy-start(bf16[768,256]{1,0:T(8,128)(2,1)} %constant.6.clone.lane_ahead) | copy-start | bytes 1179652
  35.1 22.0 %copy-start = (bf16[384,256]{1,0:T(8,128)(2,1)S(1)}, bf16[384,256]{1,0:T(8,128)(2,1)}, u32[]{:S(2)}) copy-start(bf16[384,256]{1,0:T(8,128)(2,1)} %refs_1_.1) | copy-start | bytes 589828
  35.1 22.0 %copy-start.1 = (bf16[384,256]{1,0:T(8,128)(2,1)S(1)}, bf16[384,256]{1,0:T(8,128)(2,1)}, u32[]{:S(2)}) copy-start(bf16[384,256]{1,0:T(8,128)(2,1)} %refs_2_.1) | copy-start | bytes 589828
  35.1 22.0 %copy-start.2 = (bf16[384,256]{1,0:T(8,128)(2,1)S(1)}, bf16[384,256]{1,0:T(8,128)(2,1)}, u32[]{:S(2)}) copy-start(bf16[384,256]{1,0:T(8,128)(2,1)} %refs_4_.1) | copy-start | bytes 589828
  35.1 22.0 %copy-start.3 = (bf16[384,256]{1,0:T(8,128)(2,1)S(1)}, bf16[384,256]{1,0:T(8,128)(2,1)}, u32[]{:S(2)}) copy-start(bf16[384,256]{1,0:T(8,128)(2,1)} %refs_3_.1) | copy-start | bytes 589828
  35.2 22.0 %copy-start.7 = (f32[256]{0:T(256)S(1)}, f32[256]{0:T(256)}, u32[]{:S(2)}) copy-start(f32[256]{0:T(256)} %param.13) | copy-start | bytes 3076
